TPU v7x, 1024 devices: a whole 8x8x8 slice. The times are simulated.
1024 devices in a mesh: row: 32 (over x, z_lo), col: 32 (over z_hi, y, core).
Axes of the slice: x: 8, y: 8, z: 8 (z_hi: 2, z_lo: 4; z = z_hi * 4 + z_lo), core: 2. Of those that a mesh axis runs over, the one named last changes fastest.
Arguments:
- estimate: float32 [8, 1024, 4096], P(None, 'row', 'col'), may hold values from 0.5 to 2
- views_data: bfloat16 [4, 8, 1024, 4096], P(None, None, 'row', 'col'), may hold values from 0.25 to 4
- psf_rows: float32 [4, 33], replicated, may hold values from 0.05 to 1
- psf_cols: float32 [4, 33], replicated, may hold values from 0.05 to 1
Outputs:
- estimate_next: float32 [8, 1024, 4096], P(None, 'row', 'col')
All inputs are finite; a program needn't handle non-finite values.
Results may differ from a plain program's by a relative error of at most 0.0003.
Values may be sent and summed in bfloat16 or wider, within the bound.
No kernel may reach another device: no remote copies, remote signals or barrier semaphores. Data moves between devices by JAX's collectives and lax.ppermute only.
A program may use at most 32 MiB of HBM per device.

v0:
```python
import jax
import jax.numpy as jnp
from jax import lax
from jax.sharding import PartitionSpec as P


def extended_2(shard, sides, width):
    for axis, dim in sides:
        size, length = (lax.axis_size(axis), shard.shape[dim])
        up = [(i, (i + 1) % size) for i in range(size - 1)]
        down = [(j, i) for i, j in up]
        last = lax.slice_in_dim(shard, length - width, length, axis=dim)
        leading = lax.slice_in_dim(shard, 0, width, axis=dim)
        before = lax.ppermute(last, axis, up)
        after = lax.ppermute(leading, axis, down)
        shard = jnp.concatenate([before, shard, after], axis=dim)
    return shard


def band_matrix(kernel, out_len, mirrored):
    taps = kernel.shape[0]
    row_index = lax.broadcasted_iota(jnp.int32, (out_len, out_len + taps - 1), 0)
    col_index = lax.broadcasted_iota(jnp.int32, (out_len, out_len + taps - 1), 1)
    offset = col_index - row_index
    if mirrored:
        offset = taps - 1 - offset
    tap_index = jnp.arange(taps, dtype=jnp.int32)
    matches = (offset[:, :, None] == tap_index[None, None, :]).astype(jnp.float32)
    return jnp.einsum("ijt,t->ij", matches, kernel, precision=lax.Precision.HIGHEST)


def blur_block(padded, kernel_y, kernel_x, mirrored):
    taps = kernel_y.shape[0]
    out_y = padded.shape[1] - (taps - 1)
    out_x = padded.shape[2] - (taps - 1)
    band_x = band_matrix(kernel_x, out_x, mirrored)
    band_y = band_matrix(kernel_y, out_y, mirrored)
    across = jnp.einsum("zyj,xj->zyx", padded, band_x, precision=lax.Precision.HIGHEST)
    return jnp.einsum("zjx,yj->zyx", across, band_y, precision=lax.Precision.HIGHEST)


def rim_estimate(estimate, reach):
    return extended_2(estimate.astype(jnp.bfloat16), (("row", 1), ("col", 2)), reach).astype(
        estimate.dtype
    )


def local(estimate, views_data, psf_rows, psf_cols):
    reach = (psf_rows.shape[1] - 1) // 2
    view_count = views_data.shape[0]
    kernels_y = psf_rows / jnp.sum(psf_rows, axis=1, keepdims=True)
    kernels_x = psf_cols / jnp.sum(psf_cols, axis=1, keepdims=True)
    log_sum = jnp.zeros(estimate.shape, jnp.float32)
    padded = rim_estimate(estimate, reach)
    quotients = []
    for view_index in range(view_count):
        blurred = blur_block(padded, kernels_y[view_index], kernels_x[view_index], False)
        quotients.append(views_data[view_index].astype(jnp.float32) / blurred)
    for view_index in range(view_count):
        extended = extended_2(
            quotients[view_index].astype(jnp.bfloat16), (("row", 1), ("col", 2)), reach
        ).astype(jnp.float32)
        correction = blur_block(extended, kernels_y[view_index], kernels_x[view_index], True)
        log_sum = log_sum + jnp.log(correction)
    return estimate * jnp.exp(log_sum / view_count)


def solution(mesh):
    return jax.shard_map(
        local,
        mesh=mesh,
        in_specs=(P(None, "row", "col"), P(None, None, "row", "col"), P(), P()),
        out_specs=P(None, "row", "col"),
        check_vma=False,
    )
```

profile of v0, /device:TPU:121, one launch (start us, length us, event | category | flops | bytes accessed | tf_op | source)
XLA Modules:
  0.0 143.0 jit_solution(101219457213091088)
XLA Ops:
  0.9 4.9 %collective-permute-start = (bf16[8,16,128]{2,1,0:T(8,128)(2,1)S(1)}, bf16[8,16,128]{2,1,0:T(8,128)(2,1)S(1)}, u32[]{:S(2)}, u32[]{:S(2)}) collective-permute-start(bf16[8,16,128]{2,1,0:T(8,128)(2,1)S(1)} %get-tuple-element.23), channel_id=1, source_target_pairs={{0,32},{32,64},{64,96},{96,128},{128,160},{160,192},{192,224},{224... | collective-permute-start | bytes 98312 | tf_op jit(solution)/shard_map/ppermute | solution.py:14
  5.9 7.3 %collective-permute-start.1 = (bf16[8,16,128]{2,1,0:T(8,128)(2,1)S(1)}, bf16[8,16,128]{2,1,0:T(8,128)(2,1)S(1)}, u32[]{:S(2)}, u32[]{:S(2)}) collective-permute-start(bf16[8,16,128]{2,1,0:T(8,128)(2,1)S(1)} %get-tuple-element.24), channel_id=1, source_target_pairs={{32,0},{64,32},{96,64},{128,96},{160,128},{192,160},{224,192},{256... | collective-permute-start | bytes 98312 | tf_op jit(solution)/shard_map/ppermute | solution.py:15
  16.1 1.4 fusion.25
  17.5 1.4 fusion.26
  33.5 10.8 %collective-permute-start.2 = (bf16[8,64,16]{2,1,0:T(8,128)(2,1)S(1)}, bf16[8,64,16]{2,1,0:T(8,128)(2,1)S(1)}, u32[]{:S(2)}, u32[]{:S(2)}) collective-permute-start(bf16[8,64,16]{2,1,0:T(8,128)(2,1)S(1)} %get-tuple-element.13), channel_id=1, source_target_pairs={{0,1},{1,2},{2,3},{3,4},{4,5},{5,6},{6,7},{7,8},{8,9},{9,10},{10,1... | collective-permute-start | bytes 49160 | tf_op jit(solution)/shard_map/ppermute | solution.py:14
  44.3 1.9 %collective-permute-start.3 = (bf16[8,64,16]{2,1,0:T(8,128)(2,1)S(1)}, bf16[8,64,16]{2,1,0:T(8,128)(2,1)S(1)}, u32[]{:S(2)}, u32[]{:S(2)}) collective-permute-start(bf16[8,64,16]{2,1,0:T(8,128)(2,1)S(1)} %get-tuple-element.14), channel_id=1, source_target_pairs={{1,0},{2,1},{3,2},{4,3},{5,4},{6,5},{7,6},{8,7},{9,8},{10,9},{11,1... | collective-permute-start | bytes 49160 | tf_op jit(solution)/shard_map/ppermute | solution.py:15
  47.6 9.1 %collective-permute-done.3 = bf16[8,64,16]{2,1,0:T(8,128)(2,1)S(1)} collective-permute-done((bf16[8,64,16]{2,1,0:T(8,128)(2,1)S(1)}, bf16[8,64,16]{2,1,0:T(8,128)(2,1)S(1)}, u32[]{:S(2)}, u32[]{:S(2)}) %collective-permute-start.3) | collective-permute-done | bytes 16416 | tf_op jit(solution)/shard_map/ppermute | solution.py:15
  57.6 1.9 %collective-permute-start.16 = (bf16[8,16,128]{2,1,0:T(8,128)(2,1)S(1)}, bf16[8,16,128]{2,1,0:T(8,128)(2,1)S(1)}, u32[]{:S(2)}, u32[]{:S(2)}) collective-permute-start(bf16[8,16,128]{2,1,0:T(8,128)(2,1)S(1)} %get-tuple-element.21), channel_id=1, source_target_pairs={{0,32},{32,64},{64,96},{96,128},{128,160},{160,192},{192,224},{224... | collective-permute-start | bytes 98312 | tf_op jit(solution)/shard_map/ppermute | solution.py:14
  59.5 7.3 %collective-permute-start.17 = (bf16[8,16,128]{2,1,0:T(8,128)(2,1)S(1)}, bf16[8,16,128]{2,1,0:T(8,128)(2,1)S(1)}, u32[]{:S(2)}, u32[]{:S(2)}) collective-permute-start(bf16[8,16,128]{2,1,0:T(8,128)(2,1)S(1)} %get-tuple-element.22), channel_id=1, source_target_pairs={{32,0},{64,32},{96,64},{128,96},{160,128},{192,160},{224,192},{256... | collective-permute-start | bytes 98312 | tf_op jit(solution)/shard_map/ppermute | solution.py:15
  67.4 1.9 %collective-permute-start.4 = (bf16[8,16,128]{2,1,0:T(8,128)(2,1)S(1)}, bf16[8,16,128]{2,1,0:T(8,128)(2,1)S(1)}, u32[]{:S(2)}, u32[]{:S(2)}) collective-permute-start(bf16[8,16,128]{2,1,0:T(8,128)(2,1)S(1)} %get-tuple-element.15), channel_id=1, source_target_pairs={{0,32},{32,64},{64,96},{96,128},{128,160},{160,192},{192,224},{224... | collective-permute-start | bytes 98312 | tf_op jit(solution)/shard_map/ppermute | solution.py:14
  69.3 7.3 %collective-permute-start.5 = (bf16[8,16,128]{2,1,0:T(8,128)(2,1)S(1)}, bf16[8,16,128]{2,1,0:T(8,128)(2,1)S(1)}, u32[]{:S(2)}, u32[]{:S(2)}) collective-permute-start(bf16[8,16,128]{2,1,0:T(8,128)(2,1)S(1)} %get-tuple-element.16), channel_id=1, source_target_pairs={{32,0},{64,32},{96,64},{128,96},{160,128},{192,160},{224,192},{256... | collective-permute-start | bytes 98312 | tf_op jit(solution)/shard_map/ppermute | solution.py:15
  77.7 1.9 %collective-permute-start.8 = (bf16[8,16,128]{2,1,0:T(8,128)(2,1)S(1)}, bf16[8,16,128]{2,1,0:T(8,128)(2,1)S(1)}, u32[]{:S(2)}, u32[]{:S(2)}) collective-permute-start(bf16[8,16,128]{2,1,0:T(8,128)(2,1)S(1)} %get-tuple-element.17), channel_id=1, source_target_pairs={{0,32},{32,64},{64,96},{96,128},{128,160},{160,192},{192,224},{224... | collective-permute-start | bytes 98312 | tf_op jit(solution)/shard_map/ppermute | solution.py:14
  79.9 7.3 %collective-permute-start.9 = (bf16[8,16,128]{2,1,0:T(8,128)(2,1)S(1)}, bf16[8,16,128]{2,1,0:T(8,128)(2,1)S(1)}, u32[]{:S(2)}, u32[]{:S(2)}) collective-permute-start(bf16[8,16,128]{2,1,0:T(8,128)(2,1)S(1)} %get-tuple-element.18), channel_id=1, source_target_pairs={{32,0},{64,32},{96,64},{128,96},{160,128},{192,160},{224,192},{256... | collective-permute-start | bytes 98312 | tf_op jit(solution)/shard_map/ppermute | solution.py:15
  87.2 1.9 %collective-permute-start.12 = (bf16[8,16,128]{2,1,0:T(8,128)(2,1)S(1)}, bf16[8,16,128]{2,1,0:T(8,128)(2,1)S(1)}, u32[]{:S(2)}, u32[]{:S(2)}) collective-permute-start(bf16[8,16,128]{2,1,0:T(8,128)(2,1)S(1)} %get-tuple-element.19), channel_id=1, source_target_pairs={{0,32},{32,64},{64,96},{96,128},{128,160},{160,192},{192,224},{224... | collective-permute-start | bytes 98312 | tf_op jit(solution)/shard_map/ppermute | solution.py:14
  89.2 7.3 %collective-permute-start.13 = (bf16[8,16,128]{2,1,0:T(8,128)(2,1)S(1)}, bf16[8,16,128]{2,1,0:T(8,128)(2,1)S(1)}, u32[]{:S(2)}, u32[]{:S(2)}) collective-permute-start(bf16[8,16,128]{2,1,0:T(8,128)(2,1)S(1)} %get-tuple-element.20), channel_id=1, source_target_pairs={{32,0},{64,32},{96,64},{128,96},{160,128},{192,160},{224,192},{256... | collective-permute-start | bytes 98312 | tf_op jit(solution)/shard_map/ppermute | solution.py:15
  96.5 3.9 %collective-permute-start.18 = (bf16[8,64,16]{2,1,0:T(8,128)(2,1)S(1)}, bf16[8,64,16]{2,1,0:T(8,128)(2,1)S(1)}, u32[]{:S(2)}, u32[]{:S(2)}) collective-permute-start(bf16[8,64,16]{2,1,0:T(8,128)(2,1)S(1)} %get-tuple-element.11), channel_id=1, source_target_pairs={{0,1},{1,2},{2,3},{3,4},{4,5},{5,6},{6,7},{7,8},{8,9},{9,10},{10,1... | collective-permute-start | bytes 49160 | tf_op jit(solution)/shard_map/ppermute | solution.py:14
  100.6 1.9 %collective-permute-start.19 = (bf16[8,64,16]{2,1,0:T(8,128)(2,1)S(1)}, bf16[8,64,16]{2,1,0:T(8,128)(2,1)S(1)}, u32[]{:S(2)}, u32[]{:S(2)}) collective-permute-start(bf16[8,64,16]{2,1,0:T(8,128)(2,1)S(1)} %get-tuple-element.12), channel_id=1, source_target_pairs={{1,0},{2,1},{3,2},{4,3},{5,4},{6,5},{7,6},{8,7},{9,8},{10,9},{11,1... | collective-permute-start | bytes 49160 | tf_op jit(solution)/shard_map/ppermute | solution.py:15
  102.5 9.7 %collective-permute-start.6 = (bf16[8,64,16]{2,1,0:T(8,128)(2,1)S(1)}, bf16[8,64,16]{2,1,0:T(8,128)(2,1)S(1)}, u32[]{:S(2)}, u32[]{:S(2)}) collective-permute-start(bf16[8,64,16]{2,1,0:T(8,128)(2,1)S(1)} %get-tuple-element.5), channel_id=1, source_target_pairs={{0,1},{1,2},{2,3},{3,4},{4,5},{5,6},{6,7},{7,8},{8,9},{9,10},{10,1... | collective-permute-start | bytes 49160 | tf_op jit(solution)/shard_map/ppermute | solution.py:14
  112.4 1.9 %collective-permute-start.10 = (bf16[8,64,16]{2,1,0:T(8,128)(2,1)S(1)}, bf16[8,64,16]{2,1,0:T(8,128)(2,1)S(1)}, u32[]{:S(2)}, u32[]{:S(2)}) collective-permute-start(bf16[8,64,16]{2,1,0:T(8,128)(2,1)S(1)} %get-tuple-element.7), channel_id=1, source_target_pairs={{0,1},{1,2},{2,3},{3,4},{4,5},{5,6},{6,7},{7,8},{8,9},{9,10},{10,1... | collective-permute-start | bytes 49160 | tf_op jit(solution)/shard_map/ppermute | solution.py:14
  114.3 2.4 %collective-permute-start.11 = (bf16[8,64,16]{2,1,0:T(8,128)(2,1)S(1)}, bf16[8,64,16]{2,1,0:T(8,128)(2,1)S(1)}, u32[]{:S(2)}, u32[]{:S(2)}) collective-permute-start(bf16[8,64,16]{2,1,0:T(8,128)(2,1)S(1)} %get-tuple-element.8), channel_id=1, source_target_pairs={{1,0},{2,1},{3,2},{4,3},{5,4},{6,5},{7,6},{8,7},{9,8},{10,9},{11,1... | collective-permute-start | bytes 49160 | tf_op jit(solution)/shard_map/ppermute | solution.py:15
  116.9 9.7 %collective-permute-start.14 = (bf16[8,64,16]{2,1,0:T(8,128)(2,1)S(1)}, bf16[8,64,16]{2,1,0:T(8,128)(2,1)S(1)}, u32[]{:S(2)}, u32[]{:S(2)}) collective-permute-start(bf16[8,64,16]{2,1,0:T(8,128)(2,1)S(1)} %get-tuple-element.9), channel_id=1, source_target_pairs={{0,1},{1,2},{2,3},{3,4},{4,5},{5,6},{6,7},{7,8},{8,9},{9,10},{10,1... | collective-permute-start | bytes 49160 | tf_op jit(solution)/shard_map/ppermute | solution.py:14
  126.6 1.9 %collective-permute-start.15 = (bf16[8,64,16]{2,1,0:T(8,128)(2,1)S(1)}, bf16[8,64,16]{2,1,0:T(8,128)(2,1)S(1)}, u32[]{:S(2)}, u32[]{:S(2)}) collective-permute-start(bf16[8,64,16]{2,1,0:T(8,128)(2,1)S(1)} %get-tuple-element.10), channel_id=1, source_target_pairs={{1,0},{2,1},{3,2},{4,3},{5,4},{6,5},{7,6},{8,7},{9,8},{10,9},{11,1... | collective-permute-start | bytes 49160 | tf_op jit(solution)/shard_map/ppermute | solution.py:15
  129.3 1.9 %collective-permute-start.7 = (bf16[8,64,16]{2,1,0:T(8,128)(2,1)S(1)}, bf16[8,64,16]{2,1,0:T(8,128)(2,1)S(1)}, u32[]{:S(2)}, u32[]{:S(2)}) collective-permute-start(bf16[8,64,16]{2,1,0:T(8,128)(2,1)S(1)} %get-tuple-element.6), channel_id=1, source_target_pairs={{1,0},{2,1},{3,2},{4,3},{5,4},{6,5},{7,6},{8,7},{9,8},{10,9},{11,1... | collective-permute-start | bytes 49160 | tf_op jit(solution)/shard_map/ppermute | solution.py:15
  131.2 7.7 %collective-permute-done.15 = bf16[8,64,16]{2,1,0:T(8,128)(2,1)S(1)} collective-permute-done((bf16[8,64,16]{2,1,0:T(8,128)(2,1)S(1)}, bf16[8,64,16]{2,1,0:T(8,128)(2,1)S(1)}, u32[]{:S(2)}, u32[]{:S(2)}) %collective-permute-start.15) | collective-permute-done | bytes 16416 | tf_op jit(solution)/shard_map/ppermute | solution.py:15
  (81 shorter events, 27.7 us)
Async XLA Ops:
  0.9 32.4 %collective-permute-start = (bf16[8,16,128]{2,1,0:T(8,128)(2,1)S(1)}, bf16[8,16,128]{2,1,0:T(8,128)(2,1)S(1)}, u32[]{:S(2)}, u32[]{:S(2)}) collective-permute-start(bf16[8,16,128]{2,1,0:T(8,128)(2,1)S(1)} %get-tuple-element.23), channel_id=1, source_target_pairs={{0,32},{32,64},{64,96},{96,128},{128,160},{160,192},{192,224},{224... | collective-permute-start | bytes 98312 | tf_op jit(solution)/shard_map/ppermute | solution.py:14
  5.9 27.4 %collective-permute-start.1 = (bf16[8,16,128]{2,1,0:T(8,128)(2,1)S(1)}, bf16[8,16,128]{2,1,0:T(8,128)(2,1)S(1)}, u32[]{:S(2)}, u32[]{:S(2)}) collective-permute-start(bf16[8,16,128]{2,1,0:T(8,128)(2,1)S(1)} %get-tuple-element.24), channel_id=1, source_target_pairs={{32,0},{64,32},{96,64},{128,96},{160,128},{192,160},{224,192},{256... | collective-permute-start | bytes 98312 | tf_op jit(solution)/shard_map/ppermute | solution.py:15
  17.5 5.7 %copy-start.1 = (f32[4,33]{1,0:T(4,128)S(1)}, f32[4,33]{1,0:T(4,128)}, u32[]{:S(2)}) copy-start(f32[4,33]{1,0:T(4,128)} %param.7) | copy-start | bytes 1588
  33.5 14.1 %collective-permute-start.2 = (bf16[8,64,16]{2,1,0:T(8,128)(2,1)S(1)}, bf16[8,64,16]{2,1,0:T(8,128)(2,1)S(1)}, u32[]{:S(2)}, u32[]{:S(2)}) collective-permute-start(bf16[8,64,16]{2,1,0:T(8,128)(2,1)S(1)} %get-tuple-element.13), channel_id=1, source_target_pairs={{0,1},{1,2},{2,3},{3,4},{4,5},{5,6},{6,7},{7,8},{8,9},{9,10},{10,1... | collective-permute-start | bytes 49160 | tf_op jit(solution)/shard_map/ppermute | solution.py:14
  44.3 12.4 %collective-permute-start.3 = (bf16[8,64,16]{2,1,0:T(8,128)(2,1)S(1)}, bf16[8,64,16]{2,1,0:T(8,128)(2,1)S(1)}, u32[]{:S(2)}, u32[]{:S(2)}) collective-permute-start(bf16[8,64,16]{2,1,0:T(8,128)(2,1)S(1)} %get-tuple-element.14), channel_id=1, source_target_pairs={{1,0},{2,1},{3,2},{4,3},{5,4},{6,5},{7,6},{8,7},{9,8},{10,9},{11,1... | collective-permute-start | bytes 49160 | tf_op jit(solution)/shard_map/ppermute | solution.py:15
  47.6 9.7 %copy-start.2 = (bf16[4,8,32,128]{3,2,1,0:T(8,128)(2,1)S(1)}, bf16[4,8,32,128]{3,2,1,0:T(8,128)(2,1)}, u32[]{:S(2)}) copy-start(bf16[4,8,32,128]{3,2,1,0:T(8,128)(2,1)} %param.5) | copy-start | bytes 786436
  57.6 22.3 %collective-permute-start.16 = (bf16[8,16,128]{2,1,0:T(8,128)(2,1)S(1)}, bf16[8,16,128]{2,1,0:T(8,128)(2,1)S(1)}, u32[]{:S(2)}, u32[]{:S(2)}) collective-permute-start(bf16[8,16,128]{2,1,0:T(8,128)(2,1)S(1)} %get-tuple-element.21), channel_id=1, source_target_pairs={{0,32},{32,64},{64,96},{96,128},{128,160},{160,192},{192,224},{224... | collective-permute-start | bytes 98312 | tf_op jit(solution)/shard_map/ppermute | solution.py:14
  59.5 27.7 %collective-permute-start.17 = (bf16[8,16,128]{2,1,0:T(8,128)(2,1)S(1)}, bf16[8,16,128]{2,1,0:T(8,128)(2,1)S(1)}, u32[]{:S(2)}, u32[]{:S(2)}) collective-permute-start(bf16[8,16,128]{2,1,0:T(8,128)(2,1)S(1)} %get-tuple-element.22), channel_id=1, source_target_pairs={{32,0},{64,32},{96,64},{128,96},{160,128},{192,160},{224,192},{256... | collective-permute-start | bytes 98312 | tf_op jit(solution)/shard_map/ppermute | solution.py:15
  67.4 21.8 %collective-permute-start.4 = (bf16[8,16,128]{2,1,0:T(8,128)(2,1)S(1)}, bf16[8,16,128]{2,1,0:T(8,128)(2,1)S(1)}, u32[]{:S(2)}, u32[]{:S(2)}) collective-permute-start(bf16[8,16,128]{2,1,0:T(8,128)(2,1)S(1)} %get-tuple-element.15), channel_id=1, source_target_pairs={{0,32},{32,64},{64,96},{96,128},{128,160},{160,192},{192,224},{224... | collective-permute-start | bytes 98312 | tf_op jit(solution)/shard_map/ppermute | solution.py:14
  69.3 27.2 %collective-permute-start.5 = (bf16[8,16,128]{2,1,0:T(8,128)(2,1)S(1)}, bf16[8,16,128]{2,1,0:T(8,128)(2,1)S(1)}, u32[]{:S(2)}, u32[]{:S(2)}) collective-permute-start(bf16[8,16,128]{2,1,0:T(8,128)(2,1)S(1)} %get-tuple-element.16), channel_id=1, source_target_pairs={{32,0},{64,32},{96,64},{128,96},{160,128},{192,160},{224,192},{256... | collective-permute-start | bytes 98312 | tf_op jit(solution)/shard_map/ppermute | solution.py:15
  77.7 23.0 %collective-permute-start.8 = (bf16[8,16,128]{2,1,0:T(8,128)(2,1)S(1)}, bf16[8,16,128]{2,1,0:T(8,128)(2,1)S(1)}, u32[]{:S(2)}, u32[]{:S(2)}) collective-permute-start(bf16[8,16,128]{2,1,0:T(8,128)(2,1)S(1)} %get-tuple-element.17), channel_id=1, source_target_pairs={{0,32},{32,64},{64,96},{96,128},{128,160},{160,192},{192,224},{224... | collective-permute-start | bytes 98312 | tf_op jit(solution)/shard_map/ppermute | solution.py:14
  79.9 22.7 %collective-permute-start.9 = (bf16[8,16,128]{2,1,0:T(8,128)(2,1)S(1)}, bf16[8,16,128]{2,1,0:T(8,128)(2,1)S(1)}, u32[]{:S(2)}, u32[]{:S(2)}) collective-permute-start(bf16[8,16,128]{2,1,0:T(8,128)(2,1)S(1)} %get-tuple-element.18), channel_id=1, source_target_pairs={{32,0},{64,32},{96,64},{128,96},{160,128},{192,160},{224,192},{256... | collective-permute-start | bytes 98312 | tf_op jit(solution)/shard_map/ppermute | solution.py:15
  87.2 25.2 %collective-permute-start.12 = (bf16[8,16,128]{2,1,0:T(8,128)(2,1)S(1)}, bf16[8,16,128]{2,1,0:T(8,128)(2,1)S(1)}, u32[]{:S(2)}, u32[]{:S(2)}) collective-permute-start(bf16[8,16,128]{2,1,0:T(8,128)(2,1)S(1)} %get-tuple-element.19), channel_id=1, source_target_pairs={{0,32},{32,64},{64,96},{96,128},{128,160},{160,192},{192,224},{224... | collective-permute-start | bytes 98312 | tf_op jit(solution)/shard_map/ppermute | solution.py:14
  89.2 25.0 %collective-permute-start.13 = (bf16[8,16,128]{2,1,0:T(8,128)(2,1)S(1)}, bf16[8,16,128]{2,1,0:T(8,128)(2,1)S(1)}, u32[]{:S(2)}, u32[]{:S(2)}) collective-permute-start(bf16[8,16,128]{2,1,0:T(8,128)(2,1)S(1)} %get-tuple-element.20), channel_id=1, source_target_pairs={{32,0},{64,32},{96,64},{128,96},{160,128},{192,160},{224,192},{256... | collective-permute-start | bytes 98312 | tf_op jit(solution)/shard_map/ppermute | solution.py:15
  96.5 43.1 %collective-permute-start.18 = (bf16[8,64,16]{2,1,0:T(8,128)(2,1)S(1)}, bf16[8,64,16]{2,1,0:T(8,128)(2,1)S(1)}, u32[]{:S(2)}, u32[]{:S(2)}) collective-permute-start(bf16[8,64,16]{2,1,0:T(8,128)(2,1)S(1)} %get-tuple-element.11), channel_id=1, source_target_pairs={{0,1},{1,2},{2,3},{3,4},{4,5},{5,6},{6,7},{7,8},{8,9},{9,10},{10,1... | collective-permute-start | bytes 49160 | tf_op jit(solution)/shard_map/ppermute | solution.py:14
  100.6 39.0 %collective-permute-start.19 = (bf16[8,64,16]{2,1,0:T(8,128)(2,1)S(1)}, bf16[8,64,16]{2,1,0:T(8,128)(2,1)S(1)}, u32[]{:S(2)}, u32[]{:S(2)}) collective-permute-start(bf16[8,64,16]{2,1,0:T(8,128)(2,1)S(1)} %get-tuple-element.12), channel_id=1, source_target_pairs={{1,0},{2,1},{3,2},{4,3},{5,4},{6,5},{7,6},{8,7},{9,8},{10,9},{11,1... | collective-permute-start | bytes 49160 | tf_op jit(solution)/shard_map/ppermute | solution.py:15
  102.5 37.8 %collective-permute-start.6 = (bf16[8,64,16]{2,1,0:T(8,128)(2,1)S(1)}, bf16[8,64,16]{2,1,0:T(8,128)(2,1)S(1)}, u32[]{:S(2)}, u32[]{:S(2)}) collective-permute-start(bf16[8,64,16]{2,1,0:T(8,128)(2,1)S(1)} %get-tuple-element.5), channel_id=1, source_target_pairs={{0,1},{1,2},{2,3},{3,4},{4,5},{5,6},{6,7},{7,8},{8,9},{9,10},{10,1... | collective-permute-start | bytes 49160 | tf_op jit(solution)/shard_map/ppermute | solution.py:14
  112.4 4.5 %collective-permute-start.10 = (bf16[8,64,16]{2,1,0:T(8,128)(2,1)S(1)}, bf16[8,64,16]{2,1,0:T(8,128)(2,1)S(1)}, u32[]{:S(2)}, u32[]{:S(2)}) collective-permute-start(bf16[8,64,16]{2,1,0:T(8,128)(2,1)S(1)} %get-tuple-element.7), channel_id=1, source_target_pairs={{0,1},{1,2},{2,3},{3,4},{4,5},{5,6},{6,7},{7,8},{8,9},{9,10},{10,1... | collective-permute-start | bytes 49160 | tf_op jit(solution)/shard_map/ppermute | solution.py:14
  114.3 12.3 %collective-permute-start.11 = (bf16[8,64,16]{2,1,0:T(8,128)(2,1)S(1)}, bf16[8,64,16]{2,1,0:T(8,128)(2,1)S(1)}, u32[]{:S(2)}, u32[]{:S(2)}) collective-permute-start(bf16[8,64,16]{2,1,0:T(8,128)(2,1)S(1)} %get-tuple-element.8), channel_id=1, source_target_pairs={{1,0},{2,1},{3,2},{4,3},{5,4},{6,5},{7,6},{8,7},{9,8},{10,9},{11,1... | collective-permute-start | bytes 49160 | tf_op jit(solution)/shard_map/ppermute | solution.py:15
  116.9 12.4 %collective-permute-start.14 = (bf16[8,64,16]{2,1,0:T(8,128)(2,1)S(1)}, bf16[8,64,16]{2,1,0:T(8,128)(2,1)S(1)}, u32[]{:S(2)}, u32[]{:S(2)}) collective-permute-start(bf16[8,64,16]{2,1,0:T(8,128)(2,1)S(1)} %get-tuple-element.9), channel_id=1, source_target_pairs={{0,1},{1,2},{2,3},{3,4},{4,5},{5,6},{6,7},{7,8},{8,9},{9,10},{10,1... | collective-permute-start | bytes 49160 | tf_op jit(solution)/shard_map/ppermute | solution.py:14
  126.6 12.3 %collective-permute-start.15 = (bf16[8,64,16]{2,1,0:T(8,128)(2,1)S(1)}, bf16[8,64,16]{2,1,0:T(8,128)(2,1)S(1)}, u32[]{:S(2)}, u32[]{:S(2)}) collective-permute-start(bf16[8,64,16]{2,1,0:T(8,128)(2,1)S(1)} %get-tuple-element.10), channel_id=1, source_target_pairs={{1,0},{2,1},{3,2},{4,3},{5,4},{6,5},{7,6},{8,7},{9,8},{10,9},{11,1... | collective-permute-start | bytes 49160 | tf_op jit(solution)/shard_map/ppermute | solution.py:15
  129.3 12.3 %collective-permute-start.7 = (bf16[8,64,16]{2,1,0:T(8,128)(2,1)S(1)}, bf16[8,64,16]{2,1,0:T(8,128)(2,1)S(1)}, u32[]{:S(2)}, u32[]{:S(2)}) collective-permute-start(bf16[8,64,16]{2,1,0:T(8,128)(2,1)S(1)} %get-tuple-element.6), channel_id=1, source_target_pairs={{1,0},{2,1},{3,2},{4,3},{5,4},{6,5},{7,6},{8,7},{9,8},{10,9},{11,1... | collective-permute-start | bytes 49160 | tf_op jit(solution)/shard_map/ppermute | solution.py:15
  140.4 1.6 %copy-start = (f32[8,32,128]{2,1,0:T(8,128)S(1)}, f32[8,32,128]{2,1,0:T(8,128)}, u32[]{:S(2)}) copy-start(f32[8,32,128]{2,1,0:T(8,128)} %param.4) | copy-start | bytes 393220
where the time goes:
time: 144 us; the launch traced here: 143 us
  starting transfers between devices  95.1 us (66%)
  matrix products  24.9 us (17%)
  waiting for transfers between devices  18 us (12%)
  other arithmetic  3.7 us (3%)
    ppermute x10, starting transfers between devices, extended_2(): before = lax.ppermute(last, axis, up)  48.6 us
    ppermute x10, starting transfers between devices, extended_2(): after = lax.ppermute(leading, axis, down)  46.5 us
    dot_general x16, matrix products, band_matrix(): jnp.einsum('ijt,t->ij', matches, kernel, precision=lax.Precision.HIGHEST)  18.9 us
    ppermute x10, waiting for transfers between devices, extended_2(): after = lax.ppermute(leading, axis, down)  18 us
    dot_general x8, matrix products, blur_block(): jnp.einsum('zyj,xj->zyx', padded, band_x, precision=lax.Precision.HIGHEST)  3.19 us
  transfers between devices with their start and end apart: 20, of which 3 were waited for; matrix products, arithmetic and copies ran while one was open for 18% of the time, Pallas kernels for 0%

commit v1 on v0

v1 whole, which is shorter than its diff:
```python
import functools

import jax
import jax.numpy as jnp
from jax import lax
from jax.experimental import pallas as pl
from jax.experimental.pallas import tpu as pltpu
from jax.sharding import PartitionSpec as P

F32, BF16 = jnp.float32, jnp.bfloat16
LANES = 128
WIDE = 2 * LANES


def iota(shape, dim):
    return lax.broadcasted_iota(jnp.int32, shape, dim)


def pack_kernel(dims, est_ref, views_ref, first_ref, second_ref):
    views, planes, rows, reach = dims
    odd = lax.rem(lax.axis_index("col"), 2) == 1
    wide, group = 2 * reach, LANES // (2 * reach)
    lane = iota((rows, LANES), 1)

    def strips(load, width, count):
        low = high = jnp.zeros((rows, LANES), F32)
        for k in range(count):
            block = load(k)
            here = (lane >= k * width) & (lane < (k + 1) * width)
            low = jnp.where(here, pltpu.roll(block, k * width, 1), low)
            high = jnp.where(here, pltpu.roll(block, (k + 1) * width % LANES, 1), high)
        return low, high

    def put(at, low, high):
        low, high = low.astype(BF16), high.astype(BF16)
        first_ref[at : at + rows, :] = jnp.where(odd, low, high)
        second_ref[at : at + rows, :] = jnp.where(odd, high, low)

    for t in range(planes // group):
        put(t * rows, *strips(lambda k: est_ref[t * group + k], wide, group))
    base = planes // group * rows
    for v in range(views):
        put(base + v * rows, *strips(lambda k: views_ref[v, k].astype(F32), reach, planes))


def rows_kernel(dims, est_ref, views_ref, first_ref, second_ref):
    views, planes, rows, reach = dims
    odd = lax.rem(lax.axis_index("row"), 2) == 1
    for p in range(planes):
        own = est_ref[p].astype(BF16)
        for ref in (first_ref, second_ref):
            ref[p * rows : (p + 1) * rows, :] = own
    at = planes * rows
    for v in range(views):
        for p in range(planes):
            top, bottom = views_ref[v, p, 0:reach, :], views_ref[v, p, rows - reach : rows, :]
            first_ref[at : at + reach, :] = jnp.where(odd, top, bottom)
            second_ref[at : at + reach, :] = jnp.where(odd, bottom, top)
            at += reach


def corners_kernel(dims, _1, _2, c1_ref, c2_ref, first_ref, second_ref):
    views, planes, rows, reach = dims
    odd = lax.rem(lax.axis_index("row"), 2) == 1
    strip = planes * 2 * reach // LANES * rows
    at = planes * rows + views * planes * reach
    for c in (c1_ref, c2_ref):
        for ref in (first_ref, second_ref):
            ref[at : at + strip, :] = c[0:strip, :]
        at += strip
    for c in (c1_ref, c2_ref):
        for v in range(views):
            base = strip + v * rows
            top, bottom = c[base : base + reach, :], c[base + rows - reach : base + rows, :]
            first_ref[at : at + reach, :] = jnp.where(odd, top, bottom)
            second_ref[at : at + reach, :] = jnp.where(odd, bottom, top)
            at += reach


def bands_kernel(dims, psf_y_ref, psf_x_ref, ky_ref, kx_ref, kxt_ref, kyt_ref, taps_ref):
    views, planes, rows, reach = dims
    taps = 2 * reach + 1
    tall, full = rows + 2 * reach, rows + 4 * reach
    taps_ref[...] = jnp.zeros(taps_ref.shape, F32)
    for i, ref in enumerate((psf_y_ref, psf_x_ref)):
        psf = ref[...]
        taps_ref[i, 0:views, 0:taps] = psf / jnp.sum(psf, axis=1, keepdims=True)

    def band(i, v, tap, valid):
        source = jnp.broadcast_to(taps_ref[i, v : v + 1, :], tap.shape)
        inside = valid & (tap >= 0) & (tap < taps)
        return jnp.take_along_axis(source, jnp.where(inside, tap, LANES - 1), axis=1)

    def halves(w):
        hi = w.astype(BF16)
        return hi, (w - hi.astype(F32)).astype(BF16)

    def column(j, width):
        x = jnp.where(j < LANES, j, jnp.where(j < LANES + width, j - LANES - width, j - width))
        return x, j < LANES + 2 * width

    for half in range(2):
        lanes = slice(half * LANES, (half + 1) * LANES)
        row, lane = iota((tall, LANES), 0), iota((tall, LANES), 1) + half * LANES
        for v in range(views):
            hi, lo = halves(band(0, v, lax.rem(lane, full) - row, lane < 2 * full))
            ky_ref[v * tall : (v + 1) * tall, lanes] = jnp.where(lane < full, hi.astype(F32), lo.astype(F32)).astype(BF16)
        row, lane = iota((rows, LANES), 0), iota((rows, LANES), 1) + half * LANES
        for v in range(views):
            hi, lo = halves(band(0, v, row - lax.rem(lane, tall) + 2 * reach, lane < 3 * tall))
            pick = (lane >= tall) & (lane < 2 * tall)
            kyt_ref[v * rows : (v + 1) * rows, lanes] = jnp.where(pick, lo.astype(F32), hi.astype(F32)).astype(BF16)
        shape = (WIDE, LANES)
        source, ok_source = column(iota(shape, 0), 2 * reach)
        target, ok_target = column(iota(shape, 1) + half * LANES, reach)
        tap, ok = source - target + reach, ok_source & ok_target
        for v in range(views):
            kx_ref[v, :, lanes] = band(1, v, tap, ok).astype(BF16)
    source, ok = column(iota(shape, 0), reach)
    tap = iota(shape, 1) - source + reach
    for v in range(views):
        kxt_ref[v] = band(1, v, tap, ok).astype(BF16)


def step_kernel(dims, est_ref, views_ref, c1_ref, c2_ref, r1_ref, r2_ref, ky_ref, kx_ref, kxt_ref, kyt_ref, out_ref):
    views, planes, rows, reach = dims
    wide, group = 2 * reach, LANES // (2 * reach)
    tall = rows + 2 * reach
    tiles = planes // group
    odd_col = lax.rem(lax.axis_index("col"), 2) == 1
    odd_row = lax.rem(lax.axis_index("row"), 2) == 1

    def pair(odd, one, two):
        return jnp.where(odd, one, two), jnp.where(odd, two, one)

    own = planes * rows
    at_views = own
    at_c = own + views * planes * reach
    at_cv = at_c + 2 * tiles * rows

    def edge(at, n):
        return pair(odd_row, r1_ref[at : at + n, :], r2_ref[at : at + n, :])

    blocks = []
    lane = iota((rows + 4 * reach, LANES), 1)
    halo = []
    for t in range(tiles):
        above1, below1 = edge(at_c + t * rows, rows)
        above2, below2 = edge(at_c + (tiles + t) * rows, rows)
        own1, own2 = c1_ref[t * rows : (t + 1) * rows, :], c2_ref[t * rows : (t + 1) * rows, :]
        one = jnp.concatenate([above1, own1, below1], axis=0).astype(F32)
        two = jnp.concatenate([above2, own2, below2], axis=0).astype(F32)
        halo.append(pair(odd_col, one, two))
    for p in range(planes):
        above, below = edge(p * rows, rows)
        blocks.append(jnp.concatenate([above, est_ref[p].astype(BF16), below], axis=0))
        left, right = halo[p // group]
        k = p % group
        left = pltpu.roll(left, (LANES - k * wide) % LANES, 1)
        right = pltpu.roll(right, (LANES + wide - k * wide) % LANES, 1)
        blocks.append(jnp.where(lane < wide, left, right).astype(BF16))
    field = jnp.concatenate(blocks, axis=1)
    field = jnp.concatenate([field, field, jnp.zeros((WIDE - 2 * field.shape[0], field.shape[1]), BF16)], axis=0)

    lane = iota((tall, LANES), 1)
    product = None
    every = [
        jnp.dot(ky_ref[...], field[:, p * WIDE : (p + 1) * WIDE], preferred_element_type=F32).astype(BF16)
        for p in range(planes)
    ]
    for v in range(views):
        rowed = jnp.concatenate([every[p][v * tall : (v + 1) * tall, :] for p in range(planes)], axis=0)
        blurred = jnp.dot(rowed, kx_ref[v], preferred_element_type=F32)
        above1, below1 = edge(at_cv + v * reach, reach)
        above2, below2 = edge(at_cv + (views + v) * reach, reach)
        base = tiles * rows + v * rows
        one = jnp.concatenate([above1, c1_ref[base : base + rows, :], below1], axis=0).astype(F32)
        two = jnp.concatenate([above2, c2_ref[base : base + rows, :], below2], axis=0).astype(F32)
        left, right = pair(odd_col, one, two)
        quotients = []
        for p in range(planes):
            above, below = edge(at_views + (v * planes + p) * reach, reach)
            data = jnp.concatenate([above, views_ref[v, p], below], axis=0).astype(F32)
            here = blurred[p * tall : (p + 1) * tall, :]
            main = data / here[:, :LANES]
            l = pltpu.roll(left, (LANES - p * reach) % LANES, 1)
            r = pltpu.roll(right, (LANES + reach - p * reach) % LANES, 1)
            rim = jnp.where(lane < reach, l, r) / jnp.where(lane < wide, here[:, LANES:], 1.0)
            rim = jnp.where(lane < wide, rim, 0.0)
            quotients.append(jnp.concatenate([main.astype(BF16), rim.astype(BF16)], axis=1))
        quotient = jnp.concatenate(quotients, axis=0)
        back = jnp.dot(quotient, kxt_ref[v], preferred_element_type=F32)
        hi = back.astype(BF16)
        lo = (back - hi.astype(F32)).astype(BF16)

        def planes_along_lanes(a):
            return jnp.concatenate([a[p * tall : (p + 1) * tall, :] for p in range(planes)], axis=1)

        hi, lo = planes_along_lanes(hi), planes_along_lanes(lo)
        back = jnp.concatenate([hi, hi, lo, jnp.zeros((WIDE - 3 * tall, planes * LANES), BF16)], axis=0)
        correction = jnp.dot(kyt_ref[v * rows : (v + 1) * rows, :], back, preferred_element_type=F32)
        product = correction if product is None else product * correction
    factor = jnp.sqrt(jnp.sqrt(product))
    for p in range(planes):
        out_ref[p] = est_ref[p] * factor[:, p * LANES : (p + 1) * LANES]


def swaps(size, start):
    return [pair for i in range(start, size - 1, 2) for pair in ((i, i + 1), (i + 1, i))]


def local(estimate, views_data, psf_rows, psf_cols):
    views, planes, rows, _ = views_data.shape
    reach = (psf_rows.shape[1] - 1) // 2
    dims = (views, planes, rows, reach)
    tiles = planes * 2 * reach // LANES
    strip = (tiles + views) * rows
    vmem = pl.BlockSpec(memory_space=pltpu.VMEM)
    params = pltpu.CompilerParams(vmem_limit_bytes=16 << 20)

    def call(kernel, n_in, outs, scratch=(), aliases={}):
        return pl.pallas_call(
            functools.partial(kernel, dims),
            out_shape=outs,
            in_specs=[vmem] * n_in,
            out_specs=jax.tree.map(lambda _: vmem, outs),
            scratch_shapes=scratch,
            input_output_aliases=aliases,
            compiler_params=params,
            cost_estimate=pl.CostEstimate(flops=1 << 20, bytes_accessed=1 << 20, transcendentals=0),
        )

    message = jax.ShapeDtypeStruct((strip, LANES), BF16)
    first, second = call(pack_kernel, 2, (message, message))(estimate, views_data)
    size = lax.axis_size("col")
    c1 = lax.ppermute(first, "col", swaps(size, 0))
    c2 = lax.ppermute(second, "col", swaps(size, 1))

    tall = rows + 2 * reach
    bands = call(
        bands_kernel,
        2,
        (
            jax.ShapeDtypeStruct((views * tall, WIDE), BF16),
            jax.ShapeDtypeStruct((views, WIDE, WIDE), BF16),
            jax.ShapeDtypeStruct((views, WIDE, LANES), BF16),
            jax.ShapeDtypeStruct((views * rows, WIDE), BF16),
        ),
        [pltpu.VMEM((2, 8, LANES), F32)],
    )(psf_rows, psf_cols)

    length = planes * rows + views * planes * reach + 2 * (tiles * rows + views * reach)
    message = jax.ShapeDtypeStruct((length, LANES), BF16)
    first, second = call(rows_kernel, 2, (message, message))(estimate, views_data)
    first, second = call(corners_kernel, 4, (message, message), aliases={0: 0, 1: 1})(first, second, c1, c2)
    size = lax.axis_size("row")
    r1 = lax.ppermute(first, "row", swaps(size, 0))
    r2 = lax.ppermute(second, "row", swaps(size, 1))
    return call(step_kernel, 10, jax.ShapeDtypeStruct(estimate.shape, F32))(
        estimate, views_data, c1, c2, r1, r2, *bands
    )


def solution(mesh):
    return jax.shard_map(
        local,
        mesh=mesh,
        in_specs=(P(None, "row", "col"), P(None, None, "row", "col"), P(), P()),
        out_specs=P(None, "row", "col"),
        check_vma=False,
    )
```

time: 144 us -> 37.4 us (0.26)
  starting transfers between devices: 95.1 us -> 24.9 us
  matrix products: 24.9 us -> 0 us
  waiting for transfers between devices: 18 us -> 6.26 us
  Pallas kernels: 0 us -> 3.95 us
  other arithmetic: 3.7 us -> 0 us
    ppermute x20 -> x4, starting transfers between devices: 95.1 us -> 24.9 us  [the longest x1 12.6 us: local(): c2 = lax.ppermute(second, 'col', swaps(size, 1))]
    dot_general x32 -> x0, matrix products: 24.9 us -> none  [the longest x16 18.9 us: band_matrix(): jnp.einsum('ijt,t->ij', matches, kernel, precision=lax.Precision.HIGHEST)]
    ppermute x20 -> x4, waiting for transfers between devices: 18 us -> 6.26 us  [the longest x1 4.58 us: local(): r2 = lax.ppermute(second, 'row', swaps(size, 1))]
    pallas_call x0 -> x5, Pallas kernels: none -> 3.95 us  [the longest x1 2.79 us: local(): call(step_kernel, 10, jax.ShapeDtypeStruct(estimate.shape, F32))]
    unnamed x6 -> x12, local copies, waits for them, and re-layouts: 0.01 us -> 1.87 us
  transfers between devices with their start and end apart: 20 -> 4, of which waited for: 3 -> 2; matrix products, arithmetic and copies ran while one was open for 18% -> 0% of each run, Pallas kernels for 0% -> 2%
where the time goes in v1:
time: 37.4 us; the launch traced here: 37.1 us
  starting transfers between devices  24.9 us (67%)
  waiting for transfers between devices  6.26 us (17%)
  Pallas kernels  3.95 us (11%)
  local copies, waits for them, and re-layouts  1.87 us (5%)
    ppermute x1, starting transfers between devices, local(): c2 = lax.ppermute(second, 'col', swaps(size, 1))  12.6 us
    ppermute x1, starting transfers between devices, local(): r2 = lax.ppermute(second, 'row', swaps(size, 1))  5.64 us
    ppermute x1, waiting for transfers between devices, local(): r2 = lax.ppermute(second, 'row', swaps(size, 1))  4.58 us
    ppermute x1, starting transfers between devices, local(): r1 = lax.ppermute(first, 'row', swaps(size, 0))  4.14 us
    pallas_call x1, Pallas kernels, local(): call(step_kernel, 10, jax.ShapeDtypeStruct(estimate.shape, F32))  2.79 us
    ppermute x1, starting transfers between devices, local(): c1 = lax.ppermute(first, 'col', swaps(size, 0))  2.58 us
    unnamed x12, local copies, waits for them, and re-layouts  1.87 us
    ppermute x1, waiting for transfers between devices, local(): c2 = lax.ppermute(second, 'col', swaps(size, 1))  1.68 us
  transfers between devices with their start and end apart: 4, of which 2 were waited for; matrix products, arithmetic and copies ran while one was open for 0% of the time, Pallas kernels for 2%

profile of v1, /device:TPU:121, one launch (start us, length us, event | category | flops | bytes accessed | tf_op | source)
XLA Modules:
  0.0 37.1 jit_solution(15314895015304677977)
XLA Ops:
  0.0 0.0 copy-start
  0.0 0.9 %copy-done = bf16[4,8,32,128]{3,2,1,0:T(8,128)(2,1)S(1)} copy-done((bf16[4,8,32,128]{3,2,1,0:T(8,128)(2,1)S(1)}, bf16[4,8,32,128]{3,2,1,0:T(8,128)(2,1)}, u32[]{:S(2)}) %copy-start) | copy-done | bytes 262168
  1.0 0.0 copy-start.2
  1.0 0.9 %copy-done.2 = f32[8,32,128]{2,1,0:T(8,128)S(1)} copy-done((f32[8,32,128]{2,1,0:T(8,128)S(1)}, f32[8,32,128]{2,1,0:T(8,128)}, u32[]{:S(2)}) %copy-start.2) | copy-done | bytes 131096
  1.9 0.2 shard_map.46
  2.1 2.6 %collective-permute-start = (bf16[192,128]{1,0:T(8,128)(2,1)S(1)}, bf16[192,128]{1,0:T(8,128)(2,1)S(1)}, u32[]{:S(2)}, u32[]{:S(2)}) collective-permute-start(bf16[192,128]{1,0:T(8,128)(2,1)S(1)} %get-tuple-element.15), channel_id=1, source_target_pairs={{0,1},{1,0},{2,3},{3,2},{4,5},{5,4},{6,7},{7,6},{8,9},{9,8},{10,11... | collective-permute-start | bytes 147464 | tf_op jit(solution)/shard_map/ppermute | solution.py:236
  4.7 12.6 %collective-permute-start.1 = (bf16[192,128]{1,0:T(8,128)(2,1)S(1)}, bf16[192,128]{1,0:T(8,128)(2,1)S(1)}, u32[]{:S(2)}, u32[]{:S(2)}) collective-permute-start(bf16[192,128]{1,0:T(8,128)(2,1)S(1)} %get-tuple-element.16), channel_id=1, source_target_pairs={{1,2},{2,1},{3,4},{4,3},{5,6},{6,5},{7,8},{8,7},{9,10},{10,9},{11,... | collective-permute-start | bytes 147464 | tf_op jit(solution)/shard_map/ppermute | solution.py:237
  17.3 0.1 shard_map.47
  17.3 0.0 collective-permute-done.c1_ref
  17.3 1.7 %collective-permute-done.1.c2_ref = bf16[192,128]{1,0:T(8,128)(2,1)S(1)} collective-permute-done((bf16[192,128]{1,0:T(8,128)(2,1)S(1)}, bf16[192,128]{1,0:T(8,128)(2,1)S(1)}, u32[]{:S(2)}, u32[]{:S(2)}) %collective-permute-start.1) | collective-permute-done | bytes 49184 | tf_op jit(solution)/shard_map/ppermute | solution.py:237
  19.0 0.0 copy-start.5
  19.0 0.0 copy-start.1
  19.0 0.0 copy-start.3
  19.1 0.0 copy-start.4
  19.1 4.1 %collective-permute-start.2 = (bf16[1024,128]{1,0:T(8,128)(2,1)S(1)}, bf16[1024,128]{1,0:T(8,128)(2,1)S(1)}, u32[]{:S(2)}, u32[]{:S(2)}) collective-permute-start(bf16[1024,128]{1,0:T(8,128)(2,1)S(1)} %get-tuple-element.19), channel_id=1, source_target_pairs={{0,32},{32,0},{64,96},{96,64},{128,160},{160,128},{192,224},{224,1... | collective-permute-start | bytes 786440 | tf_op jit(solution)/shard_map/ppermute | solution.py:257
  23.2 5.6 %collective-permute-start.3 = (bf16[1024,128]{1,0:T(8,128)(2,1)S(1)}, bf16[1024,128]{1,0:T(8,128)(2,1)S(1)}, u32[]{:S(2)}, u32[]{:S(2)}) collective-permute-start(bf16[1024,128]{1,0:T(8,128)(2,1)S(1)} %get-tuple-element.20), channel_id=1, source_target_pairs={{32,64},{64,32},{96,128},{128,96},{160,192},{192,160},{224,256},{2... | collective-permute-start | bytes 786440 | tf_op jit(solution)/shard_map/ppermute | solution.py:258
  28.9 0.0 copy-done.5
  28.9 0.0 copy-done.4
  28.9 0.9 %shard_map.49 = (bf16[256,256]{1,0:T(8,128)(2,1)S(1)}, bf16[4,256,256]{2,1,0:T(8,128)(2,1)S(1)}, bf16[4,256,128]{2,1,0:T(8,128)(2,1)S(1)}, bf16[128,256]{1,0:T(8,128)(2,1)S(1)}) custom-call(f32[4,33]{1,0:T(4,128)S(1)} %copy-done.4, f32[4,33]{1,0:T(4,128)S(1)} %copy-done.5), custom_call_target="tpu_custom_call" | custom-call | flops 1048576 | bytes 1048576 | tf_op jit(solution)/shard_map/pallas_call | solution.py:240
  29.8 0.0 collective-permute-done.2.r1_ref
  29.8 4.6 %collective-permute-done.3.r2_ref = bf16[1024,128]{1,0:T(8,128)(2,1)S(1)} collective-permute-done((bf16[1024,128]{1,0:T(8,128)(2,1)S(1)}, bf16[1024,128]{1,0:T(8,128)(2,1)S(1)}, u32[]{:S(2)}, u32[]{:S(2)}) %collective-permute-start.3) | collective-permute-done | bytes 262176 | tf_op jit(solution)/shard_map/ppermute | solution.py:258
  34.3 0.0 copy-done.1
  34.3 0.0 copy-done.3
  34.4 2.8 %shard_map.50 = f32[8,32,128]{2,1,0:T(8,128)} custom-call(f32[8,32,128]{2,1,0:T(8,128)S(1)} %copy-done.3, bf16[4,8,32,128]{3,2,1,0:T(8,128)(2,1)S(1)} %copy-done.1, bf16[192,128]{1,0:T(8,128)(2,1)S(1)} %collective-permute-done.c1_ref, bf16[192,128]{1,0:T(8,128)(2,1)S(1)} %collective-permute-done.1.c2_ref, ...), custom_call_target="tpu_custom_call" | custom-call | flops 1048576 | bytes 1048576 | tf_op jit(solution)/shard_map/pallas_call | solution.py:259
  (1 shorter events, 0.0 us)
Async XLA Ops:
  0.0 0.9 %copy-start = (bf16[4,8,32,128]{3,2,1,0:T(8,128)(2,1)S(1)}, bf16[4,8,32,128]{3,2,1,0:T(8,128)(2,1)}, u32[]{:S(2)}) copy-start(bf16[4,8,32,128]{3,2,1,0:T(8,128)(2,1)} %views_ref.5) | copy-start | bytes 786436
  1.0 0.9 %copy-start.2 = (f32[8,32,128]{2,1,0:T(8,128)S(1)}, f32[8,32,128]{2,1,0:T(8,128)}, u32[]{:S(2)}) copy-start(f32[8,32,128]{2,1,0:T(8,128)} %est_ref.5) | copy-start | bytes 393220
  2.1 15.2 %collective-permute-start = (bf16[192,128]{1,0:T(8,128)(2,1)S(1)}, bf16[192,128]{1,0:T(8,128)(2,1)S(1)}, u32[]{:S(2)}, u32[]{:S(2)}) collective-permute-start(bf16[192,128]{1,0:T(8,128)(2,1)S(1)} %get-tuple-element.15), channel_id=1, source_target_pairs={{0,1},{1,0},{2,3},{3,2},{4,5},{5,4},{6,7},{7,6},{8,9},{9,8},{10,11... | collective-permute-start | bytes 147464 | tf_op jit(solution)/shard_map/ppermute | solution.py:236
  4.7 14.3 %collective-permute-start.1 = (bf16[192,128]{1,0:T(8,128)(2,1)S(1)}, bf16[192,128]{1,0:T(8,128)(2,1)S(1)}, u32[]{:S(2)}, u32[]{:S(2)}) collective-permute-start(bf16[192,128]{1,0:T(8,128)(2,1)S(1)} %get-tuple-element.16), channel_id=1, source_target_pairs={{1,2},{2,1},{3,4},{4,3},{5,6},{6,5},{7,8},{8,7},{9,10},{10,9},{11,... | collective-permute-start | bytes 147464 | tf_op jit(solution)/shard_map/ppermute | solution.py:237
  19.0 9.8 %copy-start.5 = (f32[4,33]{1,0:T(4,128)S(1)}, f32[4,33]{1,0:T(4,128)}, u32[]{:S(2)}) copy-start(f32[4,33]{1,0:T(4,128)} %psf_x_ref.1) | copy-start | bytes 1588
  19.0 15.3 %copy-start.1 = (bf16[4,8,32,128]{3,2,1,0:T(8,128)(2,1)S(1)}, bf16[4,8,32,128]{3,2,1,0:T(8,128)(2,1)}, u32[]{:S(2)}) copy-start(bf16[4,8,32,128]{3,2,1,0:T(8,128)(2,1)} %views_ref.5) | copy-start | bytes 786436
  19.0 15.3 %copy-start.3 = (f32[8,32,128]{2,1,0:T(8,128)S(1)}, f32[8,32,128]{2,1,0:T(8,128)}, u32[]{:S(2)}) copy-start(f32[8,32,128]{2,1,0:T(8,128)} %est_ref.5) | copy-start | bytes 393220
  19.1 9.8 %copy-start.4 = (f32[4,33]{1,0:T(4,128)S(1)}, f32[4,33]{1,0:T(4,128)}, u32[]{:S(2)}) copy-start(f32[4,33]{1,0:T(4,128)} %psf_y_ref.1) | copy-start | bytes 1588
  19.1 10.7 %collective-permute-start.2 = (bf16[1024,128]{1,0:T(8,128)(2,1)S(1)}, bf16[1024,128]{1,0:T(8,128)(2,1)S(1)}, u32[]{:S(2)}, u32[]{:S(2)}) collective-permute-start(bf16[1024,128]{1,0:T(8,128)(2,1)S(1)} %get-tuple-element.19), channel_id=1, source_target_pairs={{0,32},{32,0},{64,96},{96,64},{128,160},{160,128},{192,224},{224,1... | collective-permute-start | bytes 786440 | tf_op jit(solution)/shard_map/ppermute | solution.py:257
  23.2 11.1 %collective-permute-start.3 = (bf16[1024,128]{1,0:T(8,128)(2,1)S(1)}, bf16[1024,128]{1,0:T(8,128)(2,1)S(1)}, u32[]{:S(2)}, u32[]{:S(2)}) collective-permute-start(bf16[1024,128]{1,0:T(8,128)(2,1)S(1)} %get-tuple-element.20), channel_id=1, source_target_pairs={{32,64},{64,32},{96,128},{128,96},{160,192},{192,160},{224,256},{2... | collective-permute-start | bytes 786440 | tf_op jit(solution)/shard_map/ppermute | solution.py:258

commit v2 on v1

v2 whole, which is shorter than its diff:
```python
import functools

import jax
import jax.numpy as jnp
from jax import lax
from jax.experimental import pallas as pl
from jax.experimental.pallas import tpu as pltpu
from jax.sharding import PartitionSpec as P

F32, BF16 = jnp.float32, jnp.bfloat16
LANES = 128
WIDE = 2 * LANES


def iota(shape, dim):
    return lax.broadcasted_iota(jnp.int32, shape, dim)


def pack_kernel(dims, est_hbm, views_hbm, low_ref, high_ref, est_ref, views_ref, sems):
    views, planes, rows, reach = dims
    wide, group = 2 * reach, LANES // (2 * reach)
    lane = iota((rows, LANES), 1)
    copies = [
        pltpu.make_async_copy(hbm, ref, sems.at[i])
        for i, (hbm, ref) in enumerate(((est_hbm, est_ref), (views_hbm, views_ref)))
    ]
    for copy in copies:
        copy.start()

    def strips(at, load, width, count):
        low = high = jnp.zeros((rows, LANES), F32)
        for k in range(count):
            block = load(k)
            here = (lane >= k * width) & (lane < (k + 1) * width)
            low = jnp.where(here, pltpu.roll(block, k * width, 1), low)
            high = jnp.where(here, pltpu.roll(block, (k + 1) * width % LANES, 1), high)
        low_ref[at : at + rows, :] = low.astype(BF16)
        high_ref[at : at + rows, :] = high.astype(BF16)

    copies[0].wait()
    for t in range(planes // group):
        strips(t * rows, lambda k: est_ref[t * group + k], wide, group)
    base = planes // group * rows
    copies[1].wait()
    for v in range(views):
        strips(base + v * rows, lambda k: views_ref[v, k].astype(F32), reach, planes)


def rows_kernel(dims, est_ref, views_ref, right_ref, left_ref, bottom_ref, top_ref):
    views, planes, rows, reach = dims
    strip = planes * 2 * reach // LANES * rows
    at = 0

    def both(block):
        for ref in (bottom_ref, top_ref):
            ref[at : at + block.shape[0], :] = block
        return at + block.shape[0]

    def sides(ref, base):
        top_ref[at : at + reach, :] = ref[base : base + reach, :]
        bottom_ref[at : at + reach, :] = ref[base + rows - reach : base + rows, :]
        return at + reach

    for p in range(planes):
        at = both(est_ref[p].astype(BF16))
    for v in range(views):
        for p in range(planes):
            at = sides(views_ref.at[v, p], 0)
    for c in (left_ref, right_ref):
        at = both(c[0:strip, :])
    for c in (left_ref, right_ref):
        for v in range(views):
            at = sides(c, strip + v * rows)


def bands_kernel(dims, psf_y_ref, psf_x_ref, ky_ref, kx_ref, kxt_ref, kyt_ref, taps_ref):
    views, planes, rows, reach = dims
    taps = 2 * reach + 1
    tall, full = rows + 2 * reach, rows + 4 * reach
    taps_ref[...] = jnp.zeros(taps_ref.shape, F32)
    for i, ref in enumerate((psf_y_ref, psf_x_ref)):
        psf = ref[...]
        taps_ref[i, 0:views, 0:taps] = psf / jnp.sum(psf, axis=1, keepdims=True)

    def band(i, v, tap, valid):
        source = jnp.broadcast_to(taps_ref[i, v : v + 1, :], tap.shape)
        inside = valid & (tap >= 0) & (tap < taps)
        return jnp.take_along_axis(source, jnp.where(inside, tap, LANES - 1), axis=1)

    def halves(w):
        hi = w.astype(BF16)
        return hi, (w - hi.astype(F32)).astype(BF16)

    def column(j, width):
        x = jnp.where(j < LANES, j, jnp.where(j < LANES + width, j - LANES - width, j - width))
        return x, j < LANES + 2 * width

    for half in range(2):
        lanes = slice(half * LANES, (half + 1) * LANES)
        row, lane = iota((tall, LANES), 0), iota((tall, LANES), 1) + half * LANES
        for v in range(views):
            hi, lo = halves(band(0, v, lax.rem(lane, full) - row, lane < 2 * full))
            ky_ref[v * tall : (v + 1) * tall, lanes] = jnp.where(lane < full, hi.astype(F32), lo.astype(F32)).astype(BF16)
        row, lane = iota((rows, LANES), 0), iota((rows, LANES), 1) + half * LANES
        for v in range(views):
            hi, lo = halves(band(0, v, row - lax.rem(lane, tall) + 2 * reach, lane < 3 * tall))
            pick = (lane >= tall) & (lane < 2 * tall)
            kyt_ref[v * rows : (v + 1) * rows, lanes] = jnp.where(pick, lo.astype(F32), hi.astype(F32)).astype(BF16)
        shape = (WIDE, LANES)
        source, ok_source = column(iota(shape, 0), 2 * reach)
        target, ok_target = column(iota(shape, 1) + half * LANES, reach)
        tap, ok = source - target + reach, ok_source & ok_target
        for v in range(views):
            kx_ref[v, :, lanes] = band(1, v, tap, ok).astype(BF16)
    source, ok = column(iota(shape, 0), reach)
    tap = iota(shape, 1) - source + reach
    for v in range(views):
        kxt_ref[v] = band(1, v, tap, ok).astype(BF16)


def step_kernel(dims, est_ref, views_ref, right_ref, left_ref, above_ref, below_ref, ky_ref, kx_ref, kxt_ref, kyt_ref, out_ref):
    views, planes, rows, reach = dims
    wide, group = 2 * reach, LANES // (2 * reach)
    tall = rows + 2 * reach
    tiles = planes // group
    own = planes * rows
    at_views = own
    at_c = own + views * planes * reach
    at_cv = at_c + 2 * tiles * rows

    def tower(at, n, own):
        return jnp.concatenate([above_ref[at : at + n, :], own, below_ref[at : at + n, :]], axis=0)

    blocks = []
    lane = iota((rows + 4 * reach, LANES), 1)
    halo = []
    for t in range(tiles):
        own = slice(t * rows, (t + 1) * rows)
        left = tower(at_c + t * rows, rows, left_ref[own, :]).astype(F32)
        right = tower(at_c + (tiles + t) * rows, rows, right_ref[own, :]).astype(F32)
        halo.append((left, right))
    for p in range(planes):
        blocks.append(tower(p * rows, rows, est_ref[p].astype(BF16)))
        left, right = halo[p // group]
        k = p % group
        left = pltpu.roll(left, (LANES - k * wide) % LANES, 1)
        right = pltpu.roll(right, (LANES + wide - k * wide) % LANES, 1)
        blocks.append(jnp.where(lane < wide, left, right).astype(BF16))
    field = jnp.concatenate(blocks, axis=1)
    field = jnp.concatenate([field, field, jnp.zeros((WIDE - 2 * field.shape[0], field.shape[1]), BF16)], axis=0)

    lane = iota((tall, LANES), 1)
    product = None
    every = [
        jnp.dot(ky_ref[...], field[:, p * WIDE : (p + 1) * WIDE], preferred_element_type=F32).astype(BF16)
        for p in range(planes)
    ]
    def blur(v):
        rowed = jnp.concatenate([every[p][v * tall : (v + 1) * tall, :] for p in range(planes)], axis=0)
        return jnp.dot(rowed, kx_ref[v], preferred_element_type=F32)

    def divide(v, blurred):
        own = slice((tiles + v) * rows, (tiles + v + 1) * rows)
        left = tower(at_cv + v * reach, reach, left_ref[own, :]).astype(F32)
        right = tower(at_cv + (views + v) * reach, reach, right_ref[own, :]).astype(F32)
        quotients = []
        for p in range(planes):
            data = tower(at_views + (v * planes + p) * reach, reach, views_ref[v, p]).astype(F32)
            here = blurred[p * tall : (p + 1) * tall, :]
            main = data / here[:, :LANES]
            l = pltpu.roll(left, (LANES - p * reach) % LANES, 1)
            r = pltpu.roll(right, (LANES + reach - p * reach) % LANES, 1)
            rim = jnp.where(lane < reach, l, r) / jnp.where(lane < wide, here[:, LANES:], 1.0)
            rim = jnp.where(lane < wide, rim, 0.0)
            quotients.append(jnp.concatenate([main.astype(BF16), rim.astype(BF16)], axis=1))
        return jnp.concatenate(quotients, axis=0)

    def planes_along_lanes(a):
        return jnp.concatenate([a[p * tall : (p + 1) * tall, :] for p in range(planes)], axis=1)

    def blur_back(v, quotient):
        back = jnp.dot(quotient, kxt_ref[v], preferred_element_type=F32)
        hi = back.astype(BF16)
        lo = (back - hi.astype(F32)).astype(BF16)
        hi, lo = planes_along_lanes(hi), planes_along_lanes(lo)
        return jnp.concatenate([hi, hi, lo, jnp.zeros((WIDE - 3 * tall, planes * LANES), BF16)], axis=0)

    def correct(v, back):
        return jnp.dot(kyt_ref[v * rows : (v + 1) * rows, :], back, preferred_element_type=F32)

    blurred = [blur(v) for v in range(views)]
    quotient = [divide(v, b) for v, b in enumerate(blurred)]
    back = [blur_back(v, q) for v, q in enumerate(quotient)]
    product = functools.reduce(jnp.multiply, [correct(v, b) for v, b in enumerate(back)])
    factor = jnp.sqrt(jnp.sqrt(product))
    for p in range(planes):
        out_ref[p] = est_ref[p] * factor[:, p * LANES : (p + 1) * LANES]


def shift(array, axis, step):
    size = lax.axis_size(axis)
    return lax.ppermute(array, axis, [(i, i + step) for i in range(size) if 0 <= i + step < size])


def local(estimate, views_data, psf_rows, psf_cols):
    views, planes, rows, _ = views_data.shape
    reach = (psf_rows.shape[1] - 1) // 2
    dims = (views, planes, rows, reach)
    tiles = planes * 2 * reach // LANES
    strip = (tiles + views) * rows
    vmem, hbm = pl.BlockSpec(memory_space=pltpu.VMEM), pl.BlockSpec(memory_space=pltpu.HBM)

    def call(kernel, in_specs, outs, scratch=(), room=16):
        return pl.pallas_call(
            functools.partial(kernel, dims),
            out_shape=outs,
            in_specs=in_specs,
            out_specs=jax.tree.map(lambda _: vmem, outs),
            scratch_shapes=scratch,
            compiler_params=pltpu.CompilerParams(vmem_limit_bytes=room << 20),
            cost_estimate=pl.CostEstimate(flops=1 << 20, bytes_accessed=1 << 20, transcendentals=0),
        )

    message = jax.ShapeDtypeStruct((strip, LANES), BF16)
    low, high = call(
        pack_kernel,
        [hbm] * 2,
        (message, message),
        [pltpu.VMEM(estimate.shape, F32), pltpu.VMEM(views_data.shape, BF16), pltpu.SemaphoreType.DMA((2,))],
    )(*(pltpu.with_memory_space_constraint(a, pltpu.HBM) for a in (estimate, views_data)))
    right = shift(low, "col", -1)
    left = shift(high, "col", 1)

    tall = rows + 2 * reach
    bands = call(
        bands_kernel,
        [vmem] * 2,
        (
            jax.ShapeDtypeStruct((views * tall, WIDE), BF16),
            jax.ShapeDtypeStruct((views, WIDE, WIDE), BF16),
            jax.ShapeDtypeStruct((views, WIDE, LANES), BF16),
            jax.ShapeDtypeStruct((views * rows, WIDE), BF16),
        ),
        [pltpu.VMEM((2, 8, LANES), F32)],
    )(psf_rows, psf_cols)

    length = planes * rows + views * planes * reach + 2 * (tiles * rows + views * reach)
    message = jax.ShapeDtypeStruct((length, LANES), BF16)
    bottom, top = call(rows_kernel, [vmem] * 4, (message, message))(estimate, views_data, right, left)
    above = shift(bottom, "row", 1)
    below = shift(top, "row", -1)
    return call(step_kernel, [vmem] * 10, jax.ShapeDtypeStruct(estimate.shape, F32))(
        estimate, views_data, right, left, above, below, *bands
    )


def solution(mesh):
    return jax.shard_map(
        local,
        mesh=mesh,
        in_specs=(P(None, "row", "col"), P(None, None, "row", "col"), P(), P()),
        out_specs=P(None, "row", "col"),
        check_vma=False,
    )
```

time: 37.4 us -> 35.7 us (0.955)
  the two profiles are of different devices: /device:TPU:121 before, /device:TPU:1 now
where the time goes in v2:
time: 35.7 us; the launch traced here: 35.5 us
  starting transfers between devices  20.6 us (58%)
  waiting for transfers between devices  10.5 us (29%)
  Pallas kernels  4.25 us (12%)
    ppermute x4, starting transfers between devices, shift(): lax.ppermute(array, axis, [(i, i + step) for i in range(size) if 0 <= i +...  20.6 us
    ppermute x4, waiting for transfers between devices, shift(): lax.ppermute(array, axis, [(i, i + step) for i in range(size) if 0 <= i +...  10.5 us
    pallas_call x1, Pallas kernels, local(): call(step_kernel, [vmem] * 10, jax.ShapeDtypeStruct(estimate.shape, F32))  2.06 us
    pallas_call x1, Pallas kernels, local(): call(pack_kernel, [hbm] * 2, (message, message), [pltpu.VMEM(estimate.sha...  1.28 us
    pallas_call x1, Pallas kernels, local(): call(bands_kernel, [vmem] * 2, (jax.ShapeDtypeStruct((views * tall, WIDE)...  0.87 us
  transfers between devices with their start and end apart: 4, of which 2 were waited for; matrix products, arithmetic and copies ran while one was open for 0% of the time, Pallas kernels for 2%

profile of v2, /device:TPU:1, one launch (start us, length us, event | category | flops | bytes accessed | tf_op | source)
XLA Modules:
  0.0 35.5 jit_solution(6463059976860039536)
XLA Ops:
  0.0 0.0 copy-start
  0.0 0.0 copy-start.1
  0.0 1.3 %shard_map.46 = (bf16[192,128]{1,0:T(8,128)(2,1)S(1)}, bf16[192,128]{1,0:T(8,128)(2,1)S(1)}) custom-call(f32[8,32,128]{2,1,0:T(8,128)} %est_ref.3, bf16[4,8,32,128]{3,2,1,0:T(8,128)(2,1)} %views_ref.3), custom_call_target="tpu_custom_call" | custom-call | flops 1048576 | bytes 1048576 | tf_op jit(solution)/shard_map/pallas_call | solution.py:225
  1.3 16.1 %collective-permute-start = (bf16[192,128]{1,0:T(8,128)(2,1)S(1)}, bf16[192,128]{1,0:T(8,128)(2,1)S(1)}, u32[]{:S(2)}, u32[]{:S(2)}) collective-permute-start(bf16[192,128]{1,0:T(8,128)(2,1)S(1)} %get-tuple-element.13), channel_id=1, source_target_pairs={{1,0},{2,1},{3,2},{4,3},{5,4},{6,5},{7,6},{8,7},{9,8},{10,9},{11,1... | collective-permute-start | bytes 147464 | tf_op jit(solution)/shard_map/ppermute | solution.py:202
  17.4 1.9 %collective-permute-start.1 = (bf16[192,128]{1,0:T(8,128)(2,1)S(1)}, bf16[192,128]{1,0:T(8,128)(2,1)S(1)}, u32[]{:S(2)}, u32[]{:S(2)}) collective-permute-start(bf16[192,128]{1,0:T(8,128)(2,1)S(1)} %get-tuple-element.14), channel_id=1, source_target_pairs={{0,1},{1,2},{2,3},{3,4},{4,5},{5,6},{6,7},{7,8},{8,9},{9,10},{10,1... | collective-permute-start | bytes 147464 | tf_op jit(solution)/shard_map/ppermute | solution.py:202
  19.3 0.0 collective-permute-done.right_ref
  19.3 1.2 %collective-permute-done.1.left_ref = bf16[192,128]{1,0:T(8,128)(2,1)S(1)} collective-permute-done((bf16[192,128]{1,0:T(8,128)(2,1)S(1)}, bf16[192,128]{1,0:T(8,128)(2,1)S(1)}, u32[]{:S(2)}, u32[]{:S(2)}) %collective-permute-start.1) | collective-permute-done | bytes 49184 | tf_op jit(solution)/shard_map/ppermute | solution.py:202
  20.5 0.0 copy-done
  20.5 0.0 copy-done.1
  20.5 0.0 copy-start.3
  20.5 0.0 copy-start.2
  20.6 1.3 %collective-permute-start.2 = (bf16[1024,128]{1,0:T(8,128)(2,1)S(1)}, bf16[1024,128]{1,0:T(8,128)(2,1)S(1)}, u32[]{:S(2)}, u32[]{:S(2)}) collective-permute-start(bf16[1024,128]{1,0:T(8,128)(2,1)S(1)} %get-tuple-element.15), channel_id=1, source_target_pairs={{0,32},{32,64},{64,96},{96,128},{128,160},{160,192},{192,224},{224... | collective-permute-start | bytes 786440 | tf_op jit(solution)/shard_map/ppermute | solution.py:202
  21.9 1.3 %collective-permute-start.3 = (bf16[1024,128]{1,0:T(8,128)(2,1)S(1)}, bf16[1024,128]{1,0:T(8,128)(2,1)S(1)}, u32[]{:S(2)}, u32[]{:S(2)}) collective-permute-start(bf16[1024,128]{1,0:T(8,128)(2,1)S(1)} %get-tuple-element.16), channel_id=1, source_target_pairs={{32,0},{64,32},{96,64},{128,96},{160,128},{192,160},{224,192},{256... | collective-permute-start | bytes 786440 | tf_op jit(solution)/shard_map/ppermute | solution.py:202
  23.2 0.0 copy-done.3
  23.2 0.0 copy-done.2
  23.2 0.9 %shard_map.48 = (bf16[256,256]{1,0:T(8,128)(2,1)S(1)}, bf16[4,256,256]{2,1,0:T(8,128)(2,1)S(1)}, bf16[4,256,128]{2,1,0:T(8,128)(2,1)S(1)}, bf16[128,256]{1,0:T(8,128)(2,1)S(1)}) custom-call(f32[4,33]{1,0:T(4,128)S(1)} %copy-done.2, f32[4,33]{1,0:T(4,128)S(1)} %copy-done.3), custom_call_target="tpu_custom_call" | custom-call | flops 1048576 | bytes 1048576 | tf_op jit(solution)/shard_map/pallas_call | solution.py:235
  24.1 9.3 %collective-permute-done.2.above_ref = bf16[1024,128]{1,0:T(8,128)(2,1)S(1)} collective-permute-done((bf16[1024,128]{1,0:T(8,128)(2,1)S(1)}, bf16[1024,128]{1,0:T(8,128)(2,1)S(1)}, u32[]{:S(2)}, u32[]{:S(2)}) %collective-permute-start.2) | collective-permute-done | bytes 262176 | tf_op jit(solution)/shard_map/ppermute | solution.py:202
  33.4 0.0 collective-permute-done.3.below_ref
  33.4 2.1 %shard_map.49 = f32[8,32,128]{2,1,0:T(8,128)} custom-call(f32[8,32,128]{2,1,0:T(8,128)S(1)} %copy-done.1, bf16[4,8,32,128]{3,2,1,0:T(8,128)(2,1)S(1)} %copy-done, bf16[192,128]{1,0:T(8,128)(2,1)S(1)} %collective-permute-done.right_ref, bf16[192,128]{1,0:T(8,128)(2,1)S(1)} %collective-permute-done.1.left_ref, ...), custom_call_target="tpu_custom_call" | custom-call | flops 1048576 | bytes 1048576 | tf_op jit(solution)/shard_map/pallas_call | solution.py:252
  (1 shorter events, 0.0 us)
Async XLA Ops:
  0.0 20.5 %copy-start = (bf16[4,8,32,128]{3,2,1,0:T(8,128)(2,1)S(1)}, bf16[4,8,32,128]{3,2,1,0:T(8,128)(2,1)}, u32[]{:S(2)}) copy-start(bf16[4,8,32,128]{3,2,1,0:T(8,128)(2,1)} %views_ref.3) | copy-start | bytes 786436
  0.0 20.5 %copy-start.1 = (f32[8,32,128]{2,1,0:T(8,128)S(1)}, f32[8,32,128]{2,1,0:T(8,128)}, u32[]{:S(2)}) copy-start(f32[8,32,128]{2,1,0:T(8,128)} %est_ref.3) | copy-start | bytes 393220
  1.3 18.0 %collective-permute-start = (bf16[192,128]{1,0:T(8,128)(2,1)S(1)}, bf16[192,128]{1,0:T(8,128)(2,1)S(1)}, u32[]{:S(2)}, u32[]{:S(2)}) collective-permute-start(bf16[192,128]{1,0:T(8,128)(2,1)S(1)} %get-tuple-element.13), channel_id=1, source_target_pairs={{1,0},{2,1},{3,2},{4,3},{5,4},{6,5},{7,6},{8,7},{9,8},{10,9},{11,1... | collective-permute-start | bytes 147464 | tf_op jit(solution)/shard_map/ppermute | solution.py:202
  17.4 3.1 %collective-permute-start.1 = (bf16[192,128]{1,0:T(8,128)(2,1)S(1)}, bf16[192,128]{1,0:T(8,128)(2,1)S(1)}, u32[]{:S(2)}, u32[]{:S(2)}) collective-permute-start(bf16[192,128]{1,0:T(8,128)(2,1)S(1)} %get-tuple-element.14), channel_id=1, source_target_pairs={{0,1},{1,2},{2,3},{3,4},{4,5},{5,6},{6,7},{7,8},{8,9},{9,10},{10,1... | collective-permute-start | bytes 147464 | tf_op jit(solution)/shard_map/ppermute | solution.py:202
  20.5 2.7 %copy-start.3 = (f32[4,33]{1,0:T(4,128)S(1)}, f32[4,33]{1,0:T(4,128)}, u32[]{:S(2)}) copy-start(f32[4,33]{1,0:T(4,128)} %psf_x_ref.1) | copy-start | bytes 1588
  20.5 2.6 %copy-start.2 = (f32[4,33]{1,0:T(4,128)S(1)}, f32[4,33]{1,0:T(4,128)}, u32[]{:S(2)}) copy-start(f32[4,33]{1,0:T(4,128)} %psf_y_ref.1) | copy-start | bytes 1588
  20.6 12.8 %collective-permute-start.2 = (bf16[1024,128]{1,0:T(8,128)(2,1)S(1)}, bf16[1024,128]{1,0:T(8,128)(2,1)S(1)}, u32[]{:S(2)}, u32[]{:S(2)}) collective-permute-start(bf16[1024,128]{1,0:T(8,128)(2,1)S(1)} %get-tuple-element.15), channel_id=1, source_target_pairs={{0,32},{32,64},{64,96},{96,128},{128,160},{160,192},{192,224},{224... | collective-permute-start | bytes 786440 | tf_op jit(solution)/shard_map/ppermute | solution.py:202
  21.9 11.5 %collective-permute-start.3 = (bf16[1024,128]{1,0:T(8,128)(2,1)S(1)}, bf16[1024,128]{1,0:T(8,128)(2,1)S(1)}, u32[]{:S(2)}, u32[]{:S(2)}) collective-permute-start(bf16[1024,128]{1,0:T(8,128)(2,1)S(1)} %get-tuple-element.16), channel_id=1, source_target_pairs={{32,0},{64,32},{96,64},{128,96},{160,128},{192,160},{224,192},{256... | collective-permute-start | bytes 786440 | tf_op jit(solution)/shard_map/ppermute | solution.py:202

commit v3 on v2

--- a/solution.py
+++ b/solution.py
@@ -30,10 +30,9 @@
     def strips(at, load, width, count):
         low = high = jnp.zeros((rows, LANES), F32)
         for k in range(count):
-            block = load(k)
-            here = (lane >= k * width) & (lane < (k + 1) * width)
-            low = jnp.where(here, pltpu.roll(block, k * width, 1), low)
-            high = jnp.where(here, pltpu.roll(block, (k + 1) * width % LANES, 1), high)
+            block = pltpu.roll(load(k), k * width, 1) if k else load(k)
+            low = jnp.where(lane // width == k, block, low)
+            high = jnp.where(lane // width == (k - 1) % count, block, high)
         low_ref[at : at + rows, :] = low.astype(BF16)
         high_ref[at : at + rows, :] = high.astype(BF16)
 
@@ -46,19 +45,21 @@
         strips(base + v * rows, lambda k: views_ref[v, k].astype(F32), reach, planes)
 
 
-def rows_kernel(dims, est_ref, views_ref, right_ref, left_ref, bottom_ref, top_ref):
+def rows_kernel(dims, est_ref, views_ref, right_ref, left_ref, first_ref, second_ref):
     views, planes, rows, reach = dims
     strip = planes * 2 * reach // LANES * rows
+    upward = swaps_rows(lax.axis_index("col")) & (lax.axis_index("row") % 2 == 0)
     at = 0
 
     def both(block):
-        for ref in (bottom_ref, top_ref):
+        for ref in (first_ref, second_ref):
             ref[at : at + block.shape[0], :] = block
         return at + block.shape[0]
 
     def sides(ref, base):
-        top_ref[at : at + reach, :] = ref[base : base + reach, :]
-        bottom_ref[at : at + reach, :] = ref[base + rows - reach : base + rows, :]
+        top, bottom = ref[base : base + reach, :], ref[base + rows - reach : base + rows, :]
+        first_ref[at : at + reach, :] = jnp.where(upward, top, bottom)
+        second_ref[at : at + reach, :] = jnp.where(upward, bottom, top)
         return at + reach
 
     for p in range(planes):
@@ -118,7 +119,7 @@
         kxt_ref[v] = band(1, v, tap, ok).astype(BF16)
 
 
-def step_kernel(dims, est_ref, views_ref, right_ref, left_ref, above_ref, below_ref, ky_ref, kx_ref, kxt_ref, kyt_ref, out_ref):
+def step_kernel(dims, est_ref, views_ref, right_ref, left_ref, first_ref, second_ref, ky_ref, kx_ref, kxt_ref, kyt_ref, out_ref):
     views, planes, rows, reach = dims
     wide, group = 2 * reach, LANES // (2 * reach)
     tall = rows + 2 * reach
@@ -128,24 +129,31 @@
     at_c = own + views * planes * reach
     at_cv = at_c + 2 * tiles * rows
 
+    turned = swaps_rows(lax.axis_index("col")) & (lax.axis_index("row") % 2 == 1)
+
     def tower(at, n, own):
-        return jnp.concatenate([above_ref[at : at + n, :], own, below_ref[at : at + n, :]], axis=0)
-
-    blocks = []
-    lane = iota((rows + 4 * reach, LANES), 1)
-    halo = []
+        first, second = first_ref[at : at + n, :], second_ref[at : at + n, :]
+        above, below = jnp.where(turned, second, first), jnp.where(turned, first, second)
+        return jnp.concatenate([above, own, below], axis=0)
+
+    def mixed(left, right, width):
+        left, right = left.astype(F32), right.astype(F32)
+        even = iota(left.shape, 1) // width % 2 == 0
+        return jnp.where(even, right, left), jnp.where(even, left, right)
+
+    def beside(tiles, k, width):
+        shift = (1 - k) * width % LANES
+        return pltpu.roll(tiles[k % 2], shift, 1) if shift else tiles[k % 2]
+
+    blocks, halo = [], []
     for t in range(tiles):
         own = slice(t * rows, (t + 1) * rows)
-        left = tower(at_c + t * rows, rows, left_ref[own, :]).astype(F32)
-        right = tower(at_c + (tiles + t) * rows, rows, right_ref[own, :]).astype(F32)
-        halo.append((left, right))
+        left = tower(at_c + t * rows, rows, left_ref[own, :])
+        right = tower(at_c + (tiles + t) * rows, rows, right_ref[own, :])
+        halo.append(mixed(left, right, wide))
     for p in range(planes):
         blocks.append(tower(p * rows, rows, est_ref[p].astype(BF16)))
-        left, right = halo[p // group]
-        k = p % group
-        left = pltpu.roll(left, (LANES - k * wide) % LANES, 1)
-        right = pltpu.roll(right, (LANES + wide - k * wide) % LANES, 1)
-        blocks.append(jnp.where(lane < wide, left, right).astype(BF16))
+        blocks.append(beside(halo[p // group], p % group, wide).astype(BF16))
     field = jnp.concatenate(blocks, axis=1)
     field = jnp.concatenate([field, field, jnp.zeros((WIDE - 2 * field.shape[0], field.shape[1]), BF16)], axis=0)
 
@@ -161,17 +169,15 @@
 
     def divide(v, blurred):
         own = slice((tiles + v) * rows, (tiles + v + 1) * rows)
-        left = tower(at_cv + v * reach, reach, left_ref[own, :]).astype(F32)
-        right = tower(at_cv + (views + v) * reach, reach, right_ref[own, :]).astype(F32)
+        left = tower(at_cv + v * reach, reach, left_ref[own, :])
+        right = tower(at_cv + (views + v) * reach, reach, right_ref[own, :])
+        rims = mixed(left, right, reach)
         quotients = []
         for p in range(planes):
             data = tower(at_views + (v * planes + p) * reach, reach, views_ref[v, p]).astype(F32)
             here = blurred[p * tall : (p + 1) * tall, :]
             main = data / here[:, :LANES]
-            l = pltpu.roll(left, (LANES - p * reach) % LANES, 1)
-            r = pltpu.roll(right, (LANES + reach - p * reach) % LANES, 1)
-            rim = jnp.where(lane < reach, l, r) / jnp.where(lane < wide, here[:, LANES:], 1.0)
-            rim = jnp.where(lane < wide, rim, 0.0)
+            rim = jnp.where(lane < wide, beside(rims, p, reach) / here[:, LANES:], 0.0)
             quotients.append(jnp.concatenate([main.astype(BF16), rim.astype(BF16)], axis=1))
         return jnp.concatenate(quotients, axis=0)
 
@@ -200,6 +206,21 @@
 def shift(array, axis, step):
     size = lax.axis_size(axis)
     return lax.ppermute(array, axis, [(i, i + step) for i in range(size) if 0 <= i + step < size])
+
+
+def swaps_rows(col):
+    return col < 2
+
+
+def along_rows(array, step):
+    rows, cols = lax.axis_size("row"), lax.axis_size("col")
+    pairs = []
+    for i in range(rows):
+        for j in range(cols):
+            move = step if not swaps_rows(j) or i % 2 == 1 else -step
+            if 0 <= i + move < rows:
+                pairs.append((i * cols + j, (i + move) * cols + j))
+    return lax.ppermute(array, ("row", "col"), pairs)
 
 
 def local(estimate, views_data, psf_rows, psf_cols):
@@ -246,11 +267,11 @@
 
     length = planes * rows + views * planes * reach + 2 * (tiles * rows + views * reach)
     message = jax.ShapeDtypeStruct((length, LANES), BF16)
-    bottom, top = call(rows_kernel, [vmem] * 4, (message, message))(estimate, views_data, right, left)
-    above = shift(bottom, "row", 1)
-    below = shift(top, "row", -1)
+    first, second = call(rows_kernel, [vmem] * 4, (message, message))(estimate, views_data, right, left)
+    first = along_rows(first, 1)
+    second = along_rows(second, -1)
     return call(step_kernel, [vmem] * 10, jax.ShapeDtypeStruct(estimate.shape, F32))(
-        estimate, views_data, right, left, above, below, *bands
+        estimate, views_data, right, left, first, second, *bands
     )
 
 

time: 35.7 us -> 34.7 us (0.972); the launches traced: 35.5 us -> 34 us
  waiting for transfers between devices: 10.5 us -> 9.16 us
    ppermute x4 -> x2, waiting for transfers between devices: 10.5 us -> 1.19 us  [shift(): lax.ppermute(array, axis, [(i, i + step) for i in range(size) if 0 <= i +...]
    ppermute x0 -> x2, waiting for transfers between devices: none -> 7.97 us  [along_rows(): return lax.ppermute(array, ('row', 'col'), pairs)]
    ppermute x0 -> x2, starting transfers between devices: none -> 2.6 us  [along_rows(): return lax.ppermute(array, ('row', 'col'), pairs)]
    ppermute x4 -> x2, starting transfers between devices: 20.6 us -> 18 us  [shift(): lax.ppermute(array, axis, [(i, i + step) for i in range(size) if 0 <= i +...]
  transfers between devices with their start and end apart: 4 -> 4, of which waited for: 2 -> 2; matrix products, arithmetic and copies ran while one was open for 0% -> 0% of each run, Pallas kernels for 2% -> 3%
where the time goes in v3:
time: 34.7 us; the launch traced here: 34 us
  starting transfers between devices  20.6 us (59%)
  waiting for transfers between devices  9.16 us (26%)
  Pallas kernels  4.15 us (12%)
    ppermute x2, starting transfers between devices, shift(): lax.ppermute(array, axis, [(i, i + step) for i in range(size) if 0 <= i +...  18 us
    ppermute x2, waiting for transfers between devices, along_rows(): return lax.ppermute(array, ('row', 'col'), pairs)  7.97 us
    ppermute x2, starting transfers between devices, along_rows(): return lax.ppermute(array, ('row', 'col'), pairs)  2.6 us
    pallas_call x1, Pallas kernels, local(): call(step_kernel, [vmem] * 10, jax.ShapeDtypeStruct(estimate.shape, F32))  1.99 us
    pallas_call x1, Pallas kernels, local(): call(pack_kernel, [hbm] * 2, (message, message), [pltpu.VMEM(estimate.sha...  1.21 us
    ppermute x2, waiting for transfers between devices, shift(): lax.ppermute(array, axis, [(i, i + step) for i in range(size) if 0 <= i +...  1.19 us
    pallas_call x1, Pallas kernels, local(): call(bands_kernel, [vmem] * 2, (jax.ShapeDtypeStruct((views * tall, WIDE)...  0.87 us
  transfers between devices with their start and end apart: 4, of which 2 were waited for; matrix products, arithmetic and copies ran while one was open for 0% of the time, Pallas kernels for 3%

profile of v3, /device:TPU:1, one launch (start us, length us, event | category | flops | bytes accessed | tf_op | source)
XLA Modules:
  0.0 34.0 jit_solution(14037142871113948303)
XLA Ops:
  0.0 0.0 copy-start
  0.0 0.0 copy-start.1
  0.0 1.2 %shard_map.46 = (bf16[192,128]{1,0:T(8,128)(2,1)S(1)}, bf16[192,128]{1,0:T(8,128)(2,1)S(1)}) custom-call(f32[8,32,128]{2,1,0:T(8,128)} %est_ref.3, bf16[4,8,32,128]{3,2,1,0:T(8,128)(2,1)} %views_ref.3), custom_call_target="tpu_custom_call" | custom-call | flops 1048576 | bytes 1048576 | tf_op jit(solution)/shard_map/pallas_call | solution.py:246
  1.2 16.1 %collective-permute-start = (bf16[192,128]{1,0:T(8,128)(2,1)S(1)}, bf16[192,128]{1,0:T(8,128)(2,1)S(1)}, u32[]{:S(2)}, u32[]{:S(2)}) collective-permute-start(bf16[192,128]{1,0:T(8,128)(2,1)S(1)} %get-tuple-element.13), channel_id=1, source_target_pairs={{1,0},{2,1},{3,2},{4,3},{5,4},{6,5},{7,6},{8,7},{9,8},{10,9},{11,1... | collective-permute-start | bytes 147464 | tf_op jit(solution)/shard_map/ppermute | solution.py:208
  17.3 1.9 %collective-permute-start.1 = (bf16[192,128]{1,0:T(8,128)(2,1)S(1)}, bf16[192,128]{1,0:T(8,128)(2,1)S(1)}, u32[]{:S(2)}, u32[]{:S(2)}) collective-permute-start(bf16[192,128]{1,0:T(8,128)(2,1)S(1)} %get-tuple-element.14), channel_id=1, source_target_pairs={{0,1},{1,2},{2,3},{3,4},{4,5},{5,6},{6,7},{7,8},{8,9},{9,10},{10,1... | collective-permute-start | bytes 147464 | tf_op jit(solution)/shard_map/ppermute | solution.py:208
  19.2 0.0 collective-permute-done.right_ref
  19.2 1.2 %collective-permute-done.1.left_ref = bf16[192,128]{1,0:T(8,128)(2,1)S(1)} collective-permute-done((bf16[192,128]{1,0:T(8,128)(2,1)S(1)}, bf16[192,128]{1,0:T(8,128)(2,1)S(1)}, u32[]{:S(2)}, u32[]{:S(2)}) %collective-permute-start.1) | collective-permute-done | bytes 49184 | tf_op jit(solution)/shard_map/ppermute | solution.py:208
  20.4 0.0 copy-done
  20.4 0.0 copy-done.1
  20.4 0.0 copy-start.3
  20.4 0.1 shard_map.47
  20.5 0.0 copy-start.2
  20.5 0.7 %collective-permute-start.2 = (bf16[1024,128]{1,0:T(8,128)(2,1)S(1)}, bf16[1024,128]{1,0:T(8,128)(2,1)S(1)}, u32[]{:S(2)}, u32[]{:S(2)}) collective-permute-start(bf16[1024,128]{1,0:T(8,128)(2,1)S(1)} %get-tuple-element.15), channel_id=1, source_target_pairs={{2,34},{3,35},{4,36},{5,37},{6,38},{7,39},{8,40},{9,41},{10,42},{1... | collective-permute-start | bytes 786440 | tf_op jit(solution)/shard_map/ppermute | solution.py:223
  21.2 1.9 %collective-permute-start.3 = (bf16[1024,128]{1,0:T(8,128)(2,1)S(1)}, bf16[1024,128]{1,0:T(8,128)(2,1)S(1)}, u32[]{:S(2)}, u32[]{:S(2)}) collective-permute-start(bf16[1024,128]{1,0:T(8,128)(2,1)S(1)} %get-tuple-element.16), channel_id=1, source_target_pairs={{0,32},{1,33},{32,0},{33,1},{34,2},{35,3},{36,4},{37,5},{38,6},{39... | collective-permute-start | bytes 786440 | tf_op jit(solution)/shard_map/ppermute | solution.py:223
  23.1 0.0 copy-done.3
  23.1 0.0 copy-done.2
  23.2 0.9 %shard_map.48 = (bf16[256,256]{1,0:T(8,128)(2,1)S(1)}, bf16[4,256,256]{2,1,0:T(8,128)(2,1)S(1)}, bf16[4,256,128]{2,1,0:T(8,128)(2,1)S(1)}, bf16[128,256]{1,0:T(8,128)(2,1)S(1)}) custom-call(f32[4,33]{1,0:T(4,128)S(1)} %copy-done.2, f32[4,33]{1,0:T(4,128)S(1)} %copy-done.3), custom_call_target="tpu_custom_call" | custom-call | flops 1048576 | bytes 1048576 | tf_op jit(solution)/shard_map/pallas_call | solution.py:256
  24.0 0.0 collective-permute-done.2.first_ref
  24.0 8.0 %collective-permute-done.3.second_ref = bf16[1024,128]{1,0:T(8,128)(2,1)S(1)} collective-permute-done((bf16[1024,128]{1,0:T(8,128)(2,1)S(1)}, bf16[1024,128]{1,0:T(8,128)(2,1)S(1)}, u32[]{:S(2)}, u32[]{:S(2)}) %collective-permute-start.3) | collective-permute-done | bytes 262176 | tf_op jit(solution)/shard_map/ppermute | solution.py:223
  32.0 2.0 %shard_map.49 = f32[8,32,128]{2,1,0:T(8,128)} custom-call(f32[8,32,128]{2,1,0:T(8,128)S(1)} %copy-done.1, bf16[4,8,32,128]{3,2,1,0:T(8,128)(2,1)S(1)} %copy-done, bf16[192,128]{1,0:T(8,128)(2,1)S(1)} %collective-permute-done.right_ref, bf16[192,128]{1,0:T(8,128)(2,1)S(1)} %collective-permute-done.1.left_ref, ...), custom_call_target="tpu_custom_call" | custom-call | flops 1048576 | bytes 1048576 | tf_op jit(solution)/shard_map/pallas_call | solution.py:273
Async XLA Ops:
  0.0 20.4 %copy-start = (bf16[4,8,32,128]{3,2,1,0:T(8,128)(2,1)S(1)}, bf16[4,8,32,128]{3,2,1,0:T(8,128)(2,1)}, u32[]{:S(2)}) copy-start(bf16[4,8,32,128]{3,2,1,0:T(8,128)(2,1)} %views_ref.3) | copy-start | bytes 786436
  0.0 20.4 %copy-start.1 = (f32[8,32,128]{2,1,0:T(8,128)S(1)}, f32[8,32,128]{2,1,0:T(8,128)}, u32[]{:S(2)}) copy-start(f32[8,32,128]{2,1,0:T(8,128)} %est_ref.3) | copy-start | bytes 393220
  1.2 18.0 %collective-permute-start = (bf16[192,128]{1,0:T(8,128)(2,1)S(1)}, bf16[192,128]{1,0:T(8,128)(2,1)S(1)}, u32[]{:S(2)}, u32[]{:S(2)}) collective-permute-start(bf16[192,128]{1,0:T(8,128)(2,1)S(1)} %get-tuple-element.13), channel_id=1, source_target_pairs={{1,0},{2,1},{3,2},{4,3},{5,4},{6,5},{7,6},{8,7},{9,8},{10,9},{11,1... | collective-permute-start | bytes 147464 | tf_op jit(solution)/shard_map/ppermute | solution.py:208
  17.3 3.1 %collective-permute-start.1 = (bf16[192,128]{1,0:T(8,128)(2,1)S(1)}, bf16[192,128]{1,0:T(8,128)(2,1)S(1)}, u32[]{:S(2)}, u32[]{:S(2)}) collective-permute-start(bf16[192,128]{1,0:T(8,128)(2,1)S(1)} %get-tuple-element.14), channel_id=1, source_target_pairs={{0,1},{1,2},{2,3},{3,4},{4,5},{5,6},{6,7},{7,8},{8,9},{9,10},{10,1... | collective-permute-start | bytes 147464 | tf_op jit(solution)/shard_map/ppermute | solution.py:208
  20.4 2.7 %copy-start.3 = (f32[4,33]{1,0:T(4,128)S(1)}, f32[4,33]{1,0:T(4,128)}, u32[]{:S(2)}) copy-start(f32[4,33]{1,0:T(4,128)} %psf_x_ref.1) | copy-start | bytes 1588
  20.5 2.6 %copy-start.2 = (f32[4,33]{1,0:T(4,128)S(1)}, f32[4,33]{1,0:T(4,128)}, u32[]{:S(2)}) copy-start(f32[4,33]{1,0:T(4,128)} %psf_y_ref.1) | copy-start | bytes 1588
  20.5 3.5 %collective-permute-start.2 = (bf16[1024,128]{1,0:T(8,128)(2,1)S(1)}, bf16[1024,128]{1,0:T(8,128)(2,1)S(1)}, u32[]{:S(2)}, u32[]{:S(2)}) collective-permute-start(bf16[1024,128]{1,0:T(8,128)(2,1)S(1)} %get-tuple-element.15), channel_id=1, source_target_pairs={{2,34},{3,35},{4,36},{5,37},{6,38},{7,39},{8,40},{9,41},{10,42},{1... | collective-permute-start | bytes 786440 | tf_op jit(solution)/shard_map/ppermute | solution.py:223
  21.2 10.8 %collective-permute-start.3 = (bf16[1024,128]{1,0:T(8,128)(2,1)S(1)}, bf16[1024,128]{1,0:T(8,128)(2,1)S(1)}, u32[]{:S(2)}, u32[]{:S(2)}) collective-permute-start(bf16[1024,128]{1,0:T(8,128)(2,1)S(1)} %get-tuple-element.16), channel_id=1, source_target_pairs={{0,32},{1,33},{32,0},{33,1},{34,2},{35,3},{36,4},{37,5},{38,6},{39... | collective-permute-start | bytes 786440 | tf_op jit(solution)/shard_map/ppermute | solution.py:223

commit v4 on v3

--- a/solution.py
+++ b/solution.py
@@ -119,7 +119,14 @@
         kxt_ref[v] = band(1, v, tap, ok).astype(BF16)
 
 
-def step_kernel(dims, est_ref, views_ref, right_ref, left_ref, first_ref, second_ref, ky_ref, kx_ref, kxt_ref, kyt_ref, out_ref):
+def step_kernel(dims, est_ref, views_ref, right_ref, left_ref, first_ref, second_ref, *refs):
+    turned = swaps_rows(lax.axis_index("col")) & (lax.axis_index("row") % 2 == 1)
+    step = functools.partial(join, dims, est_ref, views_ref, right_ref, left_ref)
+    pl.when(turned)(lambda: step(second_ref, first_ref, *refs))
+    pl.when(jnp.logical_not(turned))(lambda: step(first_ref, second_ref, *refs))
+
+
+def join(dims, est_ref, views_ref, right_ref, left_ref, above_ref, below_ref, ky_ref, kx_ref, kxt_ref, kyt_ref, out_ref, result_ref, sems):
     views, planes, rows, reach = dims
     wide, group = 2 * reach, LANES // (2 * reach)
     tall = rows + 2 * reach
@@ -129,12 +136,8 @@
     at_c = own + views * planes * reach
     at_cv = at_c + 2 * tiles * rows
 
-    turned = swaps_rows(lax.axis_index("col")) & (lax.axis_index("row") % 2 == 1)
-
     def tower(at, n, own):
-        first, second = first_ref[at : at + n, :], second_ref[at : at + n, :]
-        above, below = jnp.where(turned, second, first), jnp.where(turned, first, second)
-        return jnp.concatenate([above, own, below], axis=0)
+        return jnp.concatenate([above_ref[at : at + n, :], own, below_ref[at : at + n, :]], axis=0)
 
     def mixed(left, right, width):
         left, right = left.astype(F32), right.astype(F32)
@@ -197,10 +200,18 @@
     blurred = [blur(v) for v in range(views)]
     quotient = [divide(v, b) for v, b in enumerate(blurred)]
     back = [blur_back(v, q) for v, q in enumerate(quotient)]
-    product = functools.reduce(jnp.multiply, [correct(v, b) for v, b in enumerate(back)])
-    factor = jnp.sqrt(jnp.sqrt(product))
-    for p in range(planes):
-        out_ref[p] = est_ref[p] * factor[:, p * LANES : (p + 1) * LANES]
+    copies, part = [], planes // 2
+    for start in range(0, planes, part):
+        lanes = slice(start * LANES, (start + part) * LANES)
+        product = functools.reduce(jnp.multiply, [correct(v, b[:, lanes]) for v, b in enumerate(back)])
+        factor = jnp.sqrt(jnp.sqrt(product))
+        for p in range(part):
+            result_ref[start + p] = est_ref[start + p] * factor[:, p * LANES : (p + 1) * LANES]
+        planes_done = pl.ds(start, part)
+        copies.append(pltpu.make_async_copy(result_ref.at[planes_done], out_ref.at[planes_done], sems.at[len(copies)]))
+        copies[-1].start()
+    for copy in copies:
+        copy.wait()
 
 
 def shift(array, axis, step):
@@ -231,12 +242,12 @@
     strip = (tiles + views) * rows
     vmem, hbm = pl.BlockSpec(memory_space=pltpu.VMEM), pl.BlockSpec(memory_space=pltpu.HBM)
 
-    def call(kernel, in_specs, outs, scratch=(), room=16):
+    def call(kernel, in_specs, outs, scratch=(), room=16, out=None):
         return pl.pallas_call(
             functools.partial(kernel, dims),
             out_shape=outs,
             in_specs=in_specs,
-            out_specs=jax.tree.map(lambda _: vmem, outs),
+            out_specs=jax.tree.map(lambda _: out or vmem, outs),
             scratch_shapes=scratch,
             compiler_params=pltpu.CompilerParams(vmem_limit_bytes=room << 20),
             cost_estimate=pl.CostEstimate(flops=1 << 20, bytes_accessed=1 << 20, transcendentals=0),
@@ -270,9 +281,13 @@
     first, second = call(rows_kernel, [vmem] * 4, (message, message))(estimate, views_data, right, left)
     first = along_rows(first, 1)
     second = along_rows(second, -1)
-    return call(step_kernel, [vmem] * 10, jax.ShapeDtypeStruct(estimate.shape, F32))(
-        estimate, views_data, right, left, first, second, *bands
-    )
+    return call(
+        step_kernel,
+        [vmem] * 10,
+        jax.ShapeDtypeStruct(estimate.shape, F32),
+        [pltpu.VMEM(estimate.shape, F32), pltpu.SemaphoreType.DMA((2,))],
+        out=hbm,
+    )(estimate, views_data, right, left, first, second, *bands)
 
 
 def solution(mesh):

time: 34.7 us -> 34.6 us (level)
  no operation moved by 1% of the time
where the time goes in v4:
time: 34.6 us; the launch traced here: 34 us
  starting transfers between devices  20.6 us (60%)
  waiting for transfers between devices  9.16 us (26%)
  Pallas kernels  4.11 us (12%)
    ppermute x2, starting transfers between devices, shift(): lax.ppermute(array, axis, [(i, i + step) for i in range(size) if 0 <= i +...  18 us
    ppermute x2, waiting for transfers between devices, along_rows(): return lax.ppermute(array, ('row', 'col'), pairs)  7.97 us
    ppermute x2, starting transfers between devices, along_rows(): return lax.ppermute(array, ('row', 'col'), pairs)  2.6 us
    pallas_call x1, Pallas kernels, local(): call(step_kernel, [vmem] * 10, jax.ShapeDtypeStruct(estimate.shape, F32),...  1.96 us
    pallas_call x1, Pallas kernels, local(): call(pack_kernel, [hbm] * 2, (message, message), [pltpu.VMEM(estimate.sha...  1.21 us
    ppermute x2, waiting for transfers between devices, shift(): lax.ppermute(array, axis, [(i, i + step) for i in range(size) if 0 <= i +...  1.19 us
    pallas_call x1, Pallas kernels, local(): call(bands_kernel, [vmem] * 2, (jax.ShapeDtypeStruct((views * tall, WIDE)...  0.87 us
  transfers between devices with their start and end apart: 4, of which 2 were waited for; matrix products, arithmetic and copies ran while one was open for 0% of the time, Pallas kernels for 3%

profile of v4, /device:TPU:1, one launch (start us, length us, event | category | flops | bytes accessed | tf_op | source)
XLA Modules:
  0.0 34.0 jit_solution(6977639291160629342)
XLA Ops:
  0.0 0.0 copy-start
  0.0 0.0 copy-start.1
  0.0 1.2 %shard_map.46 = (bf16[192,128]{1,0:T(8,128)(2,1)S(1)}, bf16[192,128]{1,0:T(8,128)(2,1)S(1)}) custom-call(f32[8,32,128]{2,1,0:T(8,128)} %est_ref.3, bf16[4,8,32,128]{3,2,1,0:T(8,128)(2,1)} %views_ref.3), custom_call_target="tpu_custom_call" | custom-call | flops 1048576 | bytes 1048576 | tf_op jit(solution)/shard_map/pallas_call | solution.py:257
  1.2 16.1 %collective-permute-start = (bf16[192,128]{1,0:T(8,128)(2,1)S(1)}, bf16[192,128]{1,0:T(8,128)(2,1)S(1)}, u32[]{:S(2)}, u32[]{:S(2)}) collective-permute-start(bf16[192,128]{1,0:T(8,128)(2,1)S(1)} %get-tuple-element.13), channel_id=1, source_target_pairs={{1,0},{2,1},{3,2},{4,3},{5,4},{6,5},{7,6},{8,7},{9,8},{10,9},{11,1... | collective-permute-start | bytes 147464 | tf_op jit(solution)/shard_map/ppermute | solution.py:219
  17.3 1.9 %collective-permute-start.1 = (bf16[192,128]{1,0:T(8,128)(2,1)S(1)}, bf16[192,128]{1,0:T(8,128)(2,1)S(1)}, u32[]{:S(2)}, u32[]{:S(2)}) collective-permute-start(bf16[192,128]{1,0:T(8,128)(2,1)S(1)} %get-tuple-element.14), channel_id=1, source_target_pairs={{0,1},{1,2},{2,3},{3,4},{4,5},{5,6},{6,7},{7,8},{8,9},{9,10},{10,1... | collective-permute-start | bytes 147464 | tf_op jit(solution)/shard_map/ppermute | solution.py:219
  19.2 0.0 collective-permute-done.right_ref
  19.2 1.2 %collective-permute-done.1.left_ref = bf16[192,128]{1,0:T(8,128)(2,1)S(1)} collective-permute-done((bf16[192,128]{1,0:T(8,128)(2,1)S(1)}, bf16[192,128]{1,0:T(8,128)(2,1)S(1)}, u32[]{:S(2)}, u32[]{:S(2)}) %collective-permute-start.1) | collective-permute-done | bytes 49184 | tf_op jit(solution)/shard_map/ppermute | solution.py:219
  20.4 0.0 copy-done
  20.4 0.0 copy-done.1
  20.4 0.0 copy-start.3
  20.4 0.1 shard_map.47
  20.5 0.0 copy-start.2
  20.5 0.7 %collective-permute-start.2 = (bf16[1024,128]{1,0:T(8,128)(2,1)S(1)}, bf16[1024,128]{1,0:T(8,128)(2,1)S(1)}, u32[]{:S(2)}, u32[]{:S(2)}) collective-permute-start(bf16[1024,128]{1,0:T(8,128)(2,1)S(1)} %get-tuple-element.15), channel_id=1, source_target_pairs={{2,34},{3,35},{4,36},{5,37},{6,38},{7,39},{8,40},{9,41},{10,42},{1... | collective-permute-start | bytes 786440 | tf_op jit(solution)/shard_map/ppermute | solution.py:234
  21.2 1.9 %collective-permute-start.3 = (bf16[1024,128]{1,0:T(8,128)(2,1)S(1)}, bf16[1024,128]{1,0:T(8,128)(2,1)S(1)}, u32[]{:S(2)}, u32[]{:S(2)}) collective-permute-start(bf16[1024,128]{1,0:T(8,128)(2,1)S(1)} %get-tuple-element.16), channel_id=1, source_target_pairs={{0,32},{1,33},{32,0},{33,1},{34,2},{35,3},{36,4},{37,5},{38,6},{39... | collective-permute-start | bytes 786440 | tf_op jit(solution)/shard_map/ppermute | solution.py:234
  23.1 0.0 copy-done.3
  23.1 0.0 copy-done.2
  23.2 0.9 %shard_map.48 = (bf16[256,256]{1,0:T(8,128)(2,1)S(1)}, bf16[4,256,256]{2,1,0:T(8,128)(2,1)S(1)}, bf16[4,256,128]{2,1,0:T(8,128)(2,1)S(1)}, bf16[128,256]{1,0:T(8,128)(2,1)S(1)}) custom-call(f32[4,33]{1,0:T(4,128)S(1)} %copy-done.2, f32[4,33]{1,0:T(4,128)S(1)} %copy-done.3), custom_call_target="tpu_custom_call" | custom-call | flops 1048576 | bytes 1048576 | tf_op jit(solution)/shard_map/pallas_call | solution.py:267
  24.0 0.0 collective-permute-done.2.first_ref
  24.0 8.0 %collective-permute-done.3.second_ref = bf16[1024,128]{1,0:T(8,128)(2,1)S(1)} collective-permute-done((bf16[1024,128]{1,0:T(8,128)(2,1)S(1)}, bf16[1024,128]{1,0:T(8,128)(2,1)S(1)}, u32[]{:S(2)}, u32[]{:S(2)}) %collective-permute-start.3) | collective-permute-done | bytes 262176 | tf_op jit(solution)/shard_map/ppermute | solution.py:234
  32.0 2.0 %shard_map.49 = f32[8,32,128]{2,1,0:T(8,128)} custom-call(f32[8,32,128]{2,1,0:T(8,128)S(1)} %copy-done.1, bf16[4,8,32,128]{3,2,1,0:T(8,128)(2,1)S(1)} %copy-done, bf16[192,128]{1,0:T(8,128)(2,1)S(1)} %collective-permute-done.right_ref, bf16[192,128]{1,0:T(8,128)(2,1)S(1)} %collective-permute-done.1.left_ref, ...), custom_call_target="tpu_custom_call" | custom-call | flops 1048576 | bytes 1048576 | tf_op jit(solution)/shard_map/pallas_call | solution.py:284
Async XLA Ops:
  0.0 20.4 %copy-start = (bf16[4,8,32,128]{3,2,1,0:T(8,128)(2,1)S(1)}, bf16[4,8,32,128]{3,2,1,0:T(8,128)(2,1)}, u32[]{:S(2)}) copy-start(bf16[4,8,32,128]{3,2,1,0:T(8,128)(2,1)} %views_ref.3) | copy-start | bytes 786436
  0.0 20.4 %copy-start.1 = (f32[8,32,128]{2,1,0:T(8,128)S(1)}, f32[8,32,128]{2,1,0:T(8,128)}, u32[]{:S(2)}) copy-start(f32[8,32,128]{2,1,0:T(8,128)} %est_ref.3) | copy-start | bytes 393220
  1.2 18.0 %collective-permute-start = (bf16[192,128]{1,0:T(8,128)(2,1)S(1)}, bf16[192,128]{1,0:T(8,128)(2,1)S(1)}, u32[]{:S(2)}, u32[]{:S(2)}) collective-permute-start(bf16[192,128]{1,0:T(8,128)(2,1)S(1)} %get-tuple-element.13), channel_id=1, source_target_pairs={{1,0},{2,1},{3,2},{4,3},{5,4},{6,5},{7,6},{8,7},{9,8},{10,9},{11,1... | collective-permute-start | bytes 147464 | tf_op jit(solution)/shard_map/ppermute | solution.py:219
  17.3 3.1 %collective-permute-start.1 = (bf16[192,128]{1,0:T(8,128)(2,1)S(1)}, bf16[192,128]{1,0:T(8,128)(2,1)S(1)}, u32[]{:S(2)}, u32[]{:S(2)}) collective-permute-start(bf16[192,128]{1,0:T(8,128)(2,1)S(1)} %get-tuple-element.14), channel_id=1, source_target_pairs={{0,1},{1,2},{2,3},{3,4},{4,5},{5,6},{6,7},{7,8},{8,9},{9,10},{10,1... | collective-permute-start | bytes 147464 | tf_op jit(solution)/shard_map/ppermute | solution.py:219
  20.4 2.7 %copy-start.3 = (f32[4,33]{1,0:T(4,128)S(1)}, f32[4,33]{1,0:T(4,128)}, u32[]{:S(2)}) copy-start(f32[4,33]{1,0:T(4,128)} %psf_x_ref.1) | copy-start | bytes 1588
  20.5 2.6 %copy-start.2 = (f32[4,33]{1,0:T(4,128)S(1)}, f32[4,33]{1,0:T(4,128)}, u32[]{:S(2)}) copy-start(f32[4,33]{1,0:T(4,128)} %psf_y_ref.1) | copy-start | bytes 1588
  20.5 3.5 %collective-permute-start.2 = (bf16[1024,128]{1,0:T(8,128)(2,1)S(1)}, bf16[1024,128]{1,0:T(8,128)(2,1)S(1)}, u32[]{:S(2)}, u32[]{:S(2)}) collective-permute-start(bf16[1024,128]{1,0:T(8,128)(2,1)S(1)} %get-tuple-element.15), channel_id=1, source_target_pairs={{2,34},{3,35},{4,36},{5,37},{6,38},{7,39},{8,40},{9,41},{10,42},{1... | collective-permute-start | bytes 786440 | tf_op jit(solution)/shard_map/ppermute | solution.py:234
  21.2 10.8 %collective-permute-start.3 = (bf16[1024,128]{1,0:T(8,128)(2,1)S(1)}, bf16[1024,128]{1,0:T(8,128)(2,1)S(1)}, u32[]{:S(2)}, u32[]{:S(2)}) collective-permute-start(bf16[1024,128]{1,0:T(8,128)(2,1)S(1)} %get-tuple-element.16), channel_id=1, source_target_pairs={{0,32},{1,33},{32,0},{33,1},{34,2},{35,3},{36,4},{37,5},{38,6},{39... | collective-permute-start | bytes 786440 | tf_op jit(solution)/shard_map/ppermute | solution.py:234
